TPU v7x, 32 devices: a whole 2x2x4 slice. The times are simulated.
32 devices in a mesh: dp: 8 (over z, x), tensor: 4 (over y, core).
Axes of the slice: x: 2, y: 2, z: 4, core: 2. Of those that a mesh axis runs over, the one named last changes fastest.
Arguments:
- block_in: bfloat16 [16384, 1024], P(('dp', 'tensor')), may hold values from -6 to 6
- segments: int32 [16, 1024], P('dp'), may hold values from 0 to 4, as said below
- first_gain: float32 [1024], replicated, may hold values from 0.5 to 1.5
- first_shift: float32 [1024], replicated, may hold values from -1.25 to 1.25
- w_qkv: bfloat16 [1024, 3, 1024], P(None, None, 'tensor'), may hold values from -0.1875 to 0.1875
- qv_bias: float32 [2, 1024], P(None, 'tensor'), may hold values from -1.75 to 1.75
- w_mix: bfloat16 [1024, 1024], P('tensor'), may hold values from -0.75 to 0.75
- mix_bias: float32 [1024], replicated, may hold values from -1.25 to 1.25
- second_gain: float32 [1024], replicated, may hold values from 0.5 to 1.5
- second_shift: float32 [1024], replicated, may hold values from -1.25 to 1.25
- w_expand: bfloat16 [1024, 4096], P(None, 'tensor'), may hold values from -0.1875 to 0.1875
- expand_bias: float32 [4096], P('tensor'), may hold values from -1.75 to 1.75
- w_reduce: bfloat16 [4096, 1024], P('tensor'), may hold values from -0.125 to 0.125
- reduce_bias: float32 [1024], replicated, may hold values from -1.25 to 1.25
- out_grad: bfloat16 [16384, 1024], P(('dp', 'tensor')), may hold values from -6 to 6
Outputs:
- block_out: bfloat16 [16384, 1024], P(('dp', 'tensor'))
- in_grad: float32 [16384, 1024], P(('dp', 'tensor'))
- first_gain_grad: float32 [1024], replicated
- first_shift_grad: float32 [1024], replicated
- qkv_grad: float32 [1024, 3, 1024], P(None, None, 'tensor')
- qv_bias_grad: float32 [2, 1024], P(None, 'tensor')
- mix_grad: float32 [1024, 1024], P('tensor')
- mix_bias_grad: float32 [1024], replicated
- second_gain_grad: float32 [1024], replicated
- second_shift_grad: float32 [1024], replicated
- expand_grad: float32 [1024, 4096], P(None, 'tensor')
- expand_bias_grad: float32 [4096], P('tensor')
- reduce_grad: float32 [4096, 1024], P('tensor')
- reduce_bias_grad: float32 [1024], replicated
Inputs may be any that keep to these rules, and one draw needn't show every extreme that they name: `segments`: each row of 1024 tokens holds five documents numbered 0 to 4 in order, each a run of consecutive tokens; document 2 starts before token 256 and its last token is at position 768 or later.
All inputs are finite; a program needn't handle non-finite values.
Results may differ from a plain program's by a relative error of at most 0.014.
Values may be sent and summed in bfloat16 or wider, within the bound.
A program may use at most 192 MiB of HBM per device.

v0:
```python
import jax
import jax.numpy as jnp
from jax import lax
from jax.sharding import PartitionSpec as P

HD = 64


epsilon = 1e-05


def layer_norm(values, norm_gain, norm_shift):
    row_mean = jnp.mean(values, axis=-1, keepdims=True)
    centered = values - row_mean
    variance = jnp.mean(centered * centered, axis=-1, keepdims=True)
    return centered * lax.rsqrt(variance + epsilon) * norm_gain + norm_shift


def gelu_tanh(values):
    return jax.nn.gelu(values, approximate=True)


def contract_rows(left_mat, right_mat):
    return lax.dot_general(
        left_mat, right_mat, (((0,), (0,)), ((), ())), preferred_element_type=jnp.float32
    )


def times_transpose(left_mat, right_mat):
    return lax.dot_general(
        left_mat, right_mat, (((1,), (1,)), ((), ())), preferred_element_type=jnp.float32
    )


def body(
    block_in,
    segments,
    first_gain,
    first_shift,
    w_qkv,
    qv_bias,
    w_mix,
    mix_bias,
    second_gain,
    second_shift,
    w_expand,
    expand_bias,
    w_reduce,
    reduce_bias,
    out_grad,
):
    local_rows, width = block_in.shape
    seq_count, seq_len = segments.shape
    all_rows = seq_count * seq_len
    head_cols = w_qkv.shape[2]
    heads_here = head_cols // HD
    score_scale = HD ** (-0.5)
    block_len = min(512, seq_len)
    block_count = seq_len // block_len
    positions = jnp.arange(seq_len, dtype=jnp.int32)
    in_float = block_in.astype(jnp.float32)
    normed_one = layer_norm(in_float, first_gain, first_shift).astype(jnp.bfloat16)
    rows_one = lax.all_gather(normed_one, "tensor", axis=0, tiled=True)
    qkv_mat = w_qkv.reshape(width, 3 * head_cols)
    projected = jnp.dot(rows_one, qkv_mat, preferred_element_type=jnp.float32).reshape(
        all_rows, 3, head_cols
    )
    shape_four = (seq_count, seq_len, heads_here, HD)
    query_rows = (projected[:, 0] + qv_bias[0]).astype(jnp.bfloat16).reshape(shape_four)
    key_rows = projected[:, 1].astype(jnp.bfloat16).reshape(shape_four)
    value_rows = (projected[:, 2] + qv_bias[1]).astype(jnp.bfloat16).reshape(shape_four)

    def block_scores(index):
        row_start = index * block_len
        row_stop = row_start + block_len
        scores = (
            jnp.einsum(
                "nqhd,nkhd->nhqk",
                query_rows[:, row_start:row_stop],
                key_rows[:, :row_stop],
                preferred_element_type=jnp.float32,
            )
            * score_scale
        )
        causal = positions[row_start:row_stop, None] >= positions[None, :row_stop]
        same_doc = segments[:, row_start:row_stop, None] == segments[:, None, :row_stop]
        allowed = jnp.logical_and(causal[None], same_doc)
        return jnp.where(allowed[:, None], scores, -1e30)

    outputs = []
    log_totals = []
    for index in range(block_count):
        row_stop = (index + 1) * block_len
        scores = block_scores(index)
        row_peak = jnp.max(scores, axis=-1, keepdims=True)
        weights = jnp.exp(scores - row_peak)
        totals = jnp.sum(weights, axis=-1, keepdims=True)
        probs = (weights / totals).astype(jnp.bfloat16)
        log_totals.append(row_peak + jnp.log(totals))
        outputs.append(
            jnp.einsum(
                "nhqk,nkhd->nqhd",
                probs,
                value_rows[:, :row_stop],
                preferred_element_type=jnp.float32,
            )
        )
    attended = jnp.concatenate(outputs, axis=1).astype(jnp.bfloat16).reshape(all_rows, head_cols)
    rows_part = attended
    mixed = (
        lax.psum_scatter(
            jnp.dot(rows_part, w_mix, preferred_element_type=jnp.float32),
            "tensor",
            scatter_dimension=0,
            tiled=True,
        )
        + mix_bias
    )
    resid = in_float + mixed
    normed_two = layer_norm(resid, second_gain, second_shift).astype(jnp.bfloat16)
    rows_two = lax.all_gather(normed_two, "tensor", axis=0, tiled=True)
    pre_act = jnp.dot(rows_two, w_expand, preferred_element_type=jnp.float32) + expand_bias
    activated = gelu_tanh(pre_act).astype(jnp.bfloat16)
    rows_part = activated
    branch = (
        lax.psum_scatter(
            jnp.dot(rows_part, w_reduce, preferred_element_type=jnp.float32).astype(jnp.bfloat16),
            "tensor",
            scatter_dimension=0,
            tiled=True,
        ).astype(jnp.float32)
        + reduce_bias
    )
    block_out = (resid + branch).astype(jnp.bfloat16)
    grad_float = out_grad.astype(jnp.float32)
    grad_rows = lax.all_gather(out_grad, "tensor", axis=0, tiled=True)
    reduce_grad = contract_rows(activated, grad_rows)
    reduce_bias_grad = jnp.sum(grad_float, axis=0)
    act_grad = times_transpose(grad_rows, w_reduce)
    unused_value, gelu_back = jax.vjp(gelu_tanh, pre_act)
    pre_grad = gelu_back(act_grad)[0].astype(jnp.bfloat16)
    expand_grad = contract_rows(rows_two, pre_grad)
    expand_bias_grad = jnp.sum(pre_grad, axis=0, dtype=jnp.float32)
    rows_part = pre_grad
    normed_two_grad = lax.psum_scatter(
        times_transpose(rows_part, w_expand), "tensor", scatter_dimension=0, tiled=True
    )
    unused_second, second_back = jax.vjp(layer_norm, resid, second_gain, second_shift)
    resid_part, second_gain_grad, second_shift_grad = second_back(normed_two_grad)
    resid_grad = grad_float + resid_part
    mixed_grad = resid_grad.astype(jnp.bfloat16)
    mix_bias_grad = jnp.sum(mixed_grad, axis=0, dtype=jnp.float32)
    mixed_rows = lax.all_gather(mixed_grad, "tensor", axis=0, tiled=True)
    mix_grad = contract_rows(attended, mixed_rows)
    attended_grad = times_transpose(mixed_rows, w_mix).astype(jnp.bfloat16).reshape(shape_four)
    query_parts = []
    key_grad = jnp.zeros(shape_four, jnp.float32)
    value_grad = jnp.zeros(shape_four, jnp.float32)
    for index in range(block_count):
        row_start = index * block_len
        row_stop = row_start + block_len
        scores = block_scores(index)
        probs_full = jnp.exp(scores - log_totals[index])
        probs = probs_full.astype(jnp.bfloat16)
        grad_block = attended_grad[:, row_start:row_stop]
        value_grad = value_grad.at[:, :row_stop].add(
            jnp.einsum("nhqk,nqhd->nkhd", probs, grad_block, preferred_element_type=jnp.float32)
        )
        prob_grad = jnp.einsum(
            "nqhd,nkhd->nhqk",
            grad_block,
            value_rows[:, :row_stop],
            preferred_element_type=jnp.float32,
        )
        score_grad = (
            probs_full * (prob_grad - jnp.sum(probs_full * prob_grad, axis=-1, keepdims=True))
        ).astype(jnp.bfloat16)
        query_parts.append(
            jnp.einsum(
                "nhqk,nkhd->nqhd",
                score_grad,
                key_rows[:, :row_stop],
                preferred_element_type=jnp.float32,
            )
            * score_scale
        )
        key_grad = key_grad.at[:, :row_stop].add(
            jnp.einsum(
                "nhqk,nqhd->nkhd",
                score_grad,
                query_rows[:, row_start:row_stop],
                preferred_element_type=jnp.float32,
            )
            * score_scale
        )
    query_grad = jnp.concatenate(query_parts, axis=1)
    stacked = jnp.stack(
        [
            query_grad.reshape(all_rows, head_cols),
            key_grad.reshape(all_rows, head_cols),
            value_grad.reshape(all_rows, head_cols),
        ],
        axis=1,
    )
    qkv_rows_grad = stacked.astype(jnp.bfloat16).reshape(all_rows, 3 * head_cols)
    qkv_grad = contract_rows(rows_one, qkv_rows_grad).reshape(width, 3, head_cols)
    column_sums = jnp.sum(qkv_rows_grad.reshape(all_rows, 3, head_cols), axis=0, dtype=jnp.float32)
    qv_bias_grad = jnp.stack([column_sums[0], column_sums[2]], axis=0)
    rows_part = qkv_rows_grad
    normed_one_grad = lax.psum_scatter(
        times_transpose(rows_part, qkv_mat).astype(jnp.bfloat16),
        "tensor",
        scatter_dimension=0,
        tiled=True,
    ).astype(jnp.float32)
    unused_first, first_back = jax.vjp(layer_norm, in_float, first_gain, first_shift)
    input_part, first_gain_grad, first_shift_grad = first_back(normed_one_grad)
    in_grad = resid_grad + input_part
    qkv_grad, qv_bias_grad, mix_grad, expand_grad, expand_bias_grad, reduce_grad = lax.psum(
        (qkv_grad, qv_bias_grad, mix_grad, expand_grad, expand_bias_grad, reduce_grad), "dp"
    )
    (
        first_gain_grad,
        first_shift_grad,
        mix_bias_grad,
        second_gain_grad,
        second_shift_grad,
        reduce_bias_grad,
    ) = lax.psum(
        (
            first_gain_grad,
            first_shift_grad,
            mix_bias_grad,
            second_gain_grad,
            second_shift_grad,
            reduce_bias_grad,
        ),
        ("dp", "tensor"),
    )
    return (
        block_out,
        in_grad,
        first_gain_grad,
        first_shift_grad,
        qkv_grad,
        qv_bias_grad,
        mix_grad,
        mix_bias_grad,
        second_gain_grad,
        second_shift_grad,
        expand_grad,
        expand_bias_grad,
        reduce_grad,
        reduce_bias_grad,
    )


def solution(mesh):
    return jax.shard_map(
        body,
        mesh=mesh,
        in_specs=(
            P(("dp", "tensor"), None),
            P("dp", None),
            P(),
            P(),
            P(None, None, "tensor"),
            P(None, "tensor"),
            P("tensor", None),
            P(),
            P(),
            P(),
            P(None, "tensor"),
            P("tensor"),
            P("tensor", None),
            P(),
            P(("dp", "tensor"), None),
        ),
        out_specs=(
            P(("dp", "tensor"), None),
            P(("dp", "tensor"), None),
            P(),
            P(),
            P(None, None, "tensor"),
            P(None, "tensor"),
            P("tensor", None),
            P(),
            P(),
            P(),
            P(None, "tensor"),
            P("tensor"),
            P("tensor", None),
            P(),
        ),
        check_vma=False,
    )
```

profile of v0, /device:TPU:0, one launch (start us, length us, event | category | flops | bytes accessed | tf_op | source)
XLA Modules:
  0.0 1022.8 jit_solution(16828666472692403849)
XLA Ops:
  11.7 2.7 fusion.31
  14.6 2.6 copy.41
  20.8 30.9 %all-gather.5.cloned.1.call-done = bf16[2048,1024]{1,0:T(8,128)(2,1)} async-done(((bf16[512,1024]{1,0:T(8,128)(2,1)}), bf16[2048,1024]{1,0:T(8,128)(2,1)}) %all-gather.5.cloned.1.call-update) | async-done | bytes 4194320 | tf_op jit(solution)/shard_map/all_gather | solution.py:63
  51.7 5.7 fusion.19
  57.5 2.3 fusion.66
  61.6 2.9 copy.47
  64.5 5.4 reshape.353
  70.0 4.8 copy.45
  74.7 5.1 reshape.352
  79.8 4.8 copy.43
  86.3 6.3 fusion.71
  92.7 4.0 fusion.70
  96.9 10.5 %fusion.13 = f32[2,4,512]{2,1,0:T(4,128)S(1)} fusion(f32[2,4,512,512]{2,3,1,0:T(8,128)} %get-tuple-element.123, f32[2,4,512]{2,1,0:T(4,128)S(1)} %get-tuple-element.122), kind=kLoop, calls=%fused_computation.29 | loop fusion | flops 4190208 | bytes 8421376 | tf_op jit(solution)/shard_map/reduce_sum | solution.py:97
  107.3 4.9 fusion.49
  112.2 3.4 fusion
  115.7 3.8 fusion.48
  122.0 4.5 fusion.72
  126.6 71.8 %reduce-scatter.5.cloned.1.call-done = f32[512,1024]{1,0:T(8,128)} async-done(((f32[2048,1024]{1,0:T(8,128)}), f32[512,1024]{1,0:T(8,128)}) %reduce-scatter.5.cloned.1.call-update) | async-done | bytes 2097168 | tf_op jit(solution)/shard_map/reduce_scatter | solution.py:111
  203.9 33.8 %all-gather.7.cloned.1.call-done = bf16[2048,1024]{1,0:T(8,128)(2,1)} async-done(((bf16[512,1024]{1,0:T(8,128)(2,1)}), bf16[2048,1024]{1,0:T(8,128)(2,1)}) %all-gather.7.cloned.1.call-update) | async-done | bytes 4194320 | tf_op jit(solution)/shard_map/all_gather | solution.py:121
  237.7 11.3 %fusion.73 = f32[2048,1024]{1,0:T(8,128)} fusion(bf16[2048,1024]{1,0:T(8,128)(2,1)} %all-gather.7.cloned.1.call-done, bf16[1024,1024]{1,0:T(8,128)(2,1)} %param.37), kind=kOutput, calls=%fused_computation.130 | convolution fusion | flops 4294967296 | bytes 14680064 | tf_op jit(solution)/shard_map/dot_general | solution.py:122
  249.1 24.7 %all-gather.9.cloned.1.call-done = bf16[2048,1024]{1,0:T(8,128)(2,1)} async-done(((bf16[512,1024]{1,0:T(8,128)(2,1)}), bf16[2048,1024]{1,0:T(8,128)(2,1)}) %all-gather.9.cloned.1.call-update) | async-done | bytes 4194320 | tf_op jit(solution)/shard_map/all_gather | solution.py:136
  273.8 12.8 %convert_reduce_fusion = (f32[1024]{0:T(1024)S(1)}, bf16[2048,1024]{1,0:T(8,128)(2,1)S(1)}) fusion(f32[2048,1024]{1,0:T(8,128)} %fusion.73, f32[1024]{0:T(1024)S(1)} %copy-done.48, bf16[2048,1024]{1,0:T(8,128)(2,1)} %all-gather.9.cloned.1.call-done, bf16[1024,1024]{1,0:T(8,128)(2,1)S(1)} %copy-done), kind=kOutput, calls=%fused_computation.19 | convolution fusion | flops 4343200768 | bytes 18882560 | tf_op jit(solution)/shard_map/dot_general | solution.py:30
  286.6 2.0 copy-done.49
  288.6 6.9 fusion.74
  295.8 11.6 %convolution_convert_fusion = bf16[2048,1024]{1,0:T(8,128)(2,1)} fusion(bf16[1024,1024]{1,0:T(8,128)(2,1)S(1)} %copy-done, f32[2048,1024]{1,0:T(8,128)} %fusion.73, f32[1024]{0:T(1024)S(1)} %copy-done.48), kind=kOutput, calls=%fused_computation.41 | convolution fusion | flops 4318035968 | bytes 14684160 | tf_op jit(solution)/shard_map/dot_general | solution.py:127
  307.5 59.9 %reduce-scatter.9.cloned.1.call-done = f32[512,1024]{1,0:T(8,128)} async-done(((f32[2048,1024]{1,0:T(8,128)}), f32[512,1024]{1,0:T(8,128)}) %reduce-scatter.9.cloned.1.call-update) | async-done | bytes 2097168 | tf_op jit(solution)/shard_map/reduce_scatter | solution.py:145
  367.4 2.3 multiply_reduce_fusion.2
  369.8 45.1 %reduce-scatter.7.cloned.1.call-done = bf16[512,1024]{1,0:T(8,128)(2,1)} async-done(((bf16[2048,1024]{1,0:T(8,128)(2,1)}), bf16[512,1024]{1,0:T(8,128)(2,1)}) %reduce-scatter.7.cloned.1.call-update) | async-done | bytes 1048592 | tf_op jit(solution)/shard_map/reduce_scatter | solution.py:126
  414.9 3.7 fusion.64
  421.4 34.5 %all-gather.11.cloned.1.call-done = bf16[2048,1024]{1,0:T(8,128)(2,1)} async-done(((bf16[512,1024]{1,0:T(8,128)(2,1)}), bf16[2048,1024]{1,0:T(8,128)(2,1)}) %all-gather.11.cloned.1.call-update) | async-done | bytes 4194320 | tf_op jit(solution)/shard_map/all_gather | solution.py:153
  455.9 4.5 convolution_convert_fusion.1
  460.4 3.7 reshape.358
  464.1 2.0 fusion.67
  467.7 5.9 fusion.38
  473.6 4.6 multiply_reduce_fusion.1
  478.3 2.4 multiply_convert_fusion.1
  482.3 2.4 fusion.41
  484.7 2.3 copy.87
  487.0 11.6 %multiply_reduce_fusion = (f32[2,4,512]{2,1,0:T(4,128)S(1)}, f32[2,4,512,1024]{3,2,1,0:T(8,128)}) fusion(f32[2,4,512,1024]{3,2,1,0:T(8,128)} %copy-done.2, f32[2,4,512]{2,1,0:T(4,128)S(1)} %bitcast.90, bf16[2,512,4,64]{1,3,2,0:T(8,128)(2,1)} %copy.87, bf16[2,1024,4,64]{1,3,2,0:T(8,128)(2,1)} %copy-done.16), kind=kOutput, calls=%fused_computation.1 | convolution fusion | flops 549449728 | bytes 35160064 | tf_op jit(solution)/shard_map/nqhd,nkhd->nhqk/dot_general | solution.py:169
  498.6 8.5 bitcast_add_fusion
  507.1 4.0 copy.77
  511.2 4.3 reshape.356
  515.5 11.9 %multiply_convert_fusion = bf16[2,4,512,1024]{3,2,1,0:T(8,128)(2,1)S(1)} fusion(f32[2,4,512,1024]{3,2,1,0:T(8,128)} %get-tuple-element.127, f32[2,4,512,1024]{3,2,1,0:T(8,128)} %copy-done.2, f32[2,4,512]{2,1,0:T(4,128)S(1)} %get-tuple-element.126, f32[2,4,512]{2,1,0:T(4,128)S(1)} %bitcast.92), kind=kLoop, calls=%fused_computation | loop fusion | flops 16777216 | bytes 41975808 | tf_op jit(solution)/shard_map/convert_element_type | solution.py:177
  527.4 2.7 fusion.43
  530.1 2.5 bitcast_add_fusion.1
  533.7 2.9 copy.75
  536.6 2.2 reshape.354
  538.8 2.9 copy.76
  541.7 2.2 reshape.355
  543.9 2.4 convert_reduce_fusion.1
  547.9 5.1 bitcast_convert_fusion
  553.3 10.1 fusion.76
  563.4 11.7 %fusion.61 = f32[1024,1024]{1,0:T(8,128)} fusion(bf16[2048,1024]{1,0:T(8,128)(2,1)S(1)} %copy-done.46, f32[2048,1024]{1,0:T(8,128)} %fusion.73, f32[1024]{0:T(1024)S(1)} %copy-done.48), kind=kOutput, calls=%fused_computation.120 | convolution fusion | flops 4315938816 | bytes 16781312 | tf_op jit(solution)/shard_map/dot_general | solution.py:24
  575.1 5.0 copy.64
  580.1 4.6 fusion.75
  584.7 5.2 fusion.17
  590.0 22.5 %all-reduce.3 = (f32[2,256]{1,0:T(2,128)}, f32[1024]{0:T(1024)}) all-reduce(f32[2,256]{1,0:T(2,128)S(1)} %pad_maximum_fusion.2, f32[1024]{0:T(1024)S(1)} %get-tuple-element.99), channel_id=1, replica_groups=mesh['dp'=8,'tensor'=4] {'dp'}, use_global_device_ids=true, to_apply=%region_24.25 | all-reduce | flops 1536 | bytes 12288 | tf_op jit(solution)/shard_map/psum | solution.py:219
  614.5 2.4 fusion.34
  617.0 3.4 convert_reduce_fusion.4
  620.4 42.3 %all-reduce.2 = (f32[1024]{0:T(1024)}, f32[1024]{0:T(1024)}, f32[1024]{0:T(1024)}, f32[1024]{0:T(1024)}, f32[1024]{0:T(1024)}, /*index=5*/f32[1024]{0:T(1024)}) all-reduce(f32[1024]{0:T(1024)S(1)} %get-tuple-element.80, f32[1024]{0:T(1024)S(1)} %get-tuple-element.83, ...), channel_id=1, replica_groups=mesh['dp'=8,'tensor'=4] {'dp','tensor'}, use_global_device_ids=true, to_apply=%region_19.20 | all-reduce | flops 6144 | bytes 49152 | tf_op jit(solution)/shard_map/psum | solution.py:229
  662.6 342.5 %all-reduce.7.cloned.1.call-done = (f32[1024,3,256]{2,0,1:T(8,128)}, f32[256,1024]{1,0:T(8,128)}, f32[1024,1024]{1,0:T(8,128)}, f32[1024,1024]{1,0:T(8,128)}) async-done(((f32[1024,3,256]{2,0,1:T(8,128)}, f32[256,1024]{1,0:T(8,128)}, f32[1024,1024]{1,0:T(8,128)}, f32[1024,1024]{1,0:T(8,128)}), (f32[1024,3,256]{2,0,1:T(8,128)}, f32[256,1024]{1,0:T(8,128)}, f32[1024,1024]{1,0:T(8,128)}, ...) | async-done | bytes 12582928 | tf_op jit(solution)/shard_map/psum | solution.py:219
  1005.2 3.9 copy.93
  1010.1 2.1 copy.95
  1013.8 2.0 copy.96
  (165 shorter events, 34.2 us)
Async XLA Ops:
  7.2 266.6 %copy-start = (bf16[1024,1024]{1,0:T(8,128)(2,1)S(1)}, bf16[1024,1024]{1,0:T(8,128)(2,1)}, u32[]{:S(2)}) copy-start(bf16[1024,1024]{1,0:T(8,128)(2,1)} %param.39) | copy-start | bytes 6291460
  7.2 7.2 copy-start.44
  7.2 10.0 copy-start.36
  7.2 44.5 %all-gather.5.cloned.1.call-start = ((), (), s32[]{:S(2)}) async-start(), calls=%async_computation.4 | async-start | bytes 5242880 | tf_op jit(solution)/shard_map/all_gather | solution.py:63
  8.8 2.2 copy-start.32
  10.5 0.6 copy-start.39
  11.1 0.6 copy-start.37
  14.3 184.1 %reduce-scatter.5.cloned.1.call-start = ((), (), s32[]{:S(2)}) async-start(), calls=%async_computation.5 | async-start | bytes 10485760 | tf_op jit(solution)/shard_map/reduce_scatter | solution.py:111
  64.5 28.1 %copy-start.8 = (bf16[2,1024,4,64]{1,3,2,0:T(8,128)(2,1)}, bf16[2,1024,4,64]{1,3,2,0:T(8,128)(2,1)S(1)}, u32[]{:S(2)}) copy-start(bf16[2,1024,4,64]{1,3,2,0:T(8,128)(2,1)S(1)} %copy.47) | copy-start | bytes 3145732
  86.3 6.4 copy-start.14
  86.3 6.4 copy-start.22
  92.7 4.0 copy-start.13
  96.7 19.0 %copy-start.2 = (f32[2,4,512,1024]{3,2,1,0:T(8,128)}, f32[2,4,512,1024]{3,2,1,0:T(8,128)S(1)}, u32[]{:S(2)}) copy-start(f32[2,4,512,1024]{3,2,1,0:T(8,128)S(1)} %get-tuple-element.121) | copy-start | bytes 50331652
  96.9 18.8 %copy-start.16 = (bf16[2,1024,4,64]{1,3,2,0:T(8,128)(2,1)}, bf16[2,1024,4,64]{1,3,2,0:T(8,128)(2,1)S(1)}, u32[]{:S(2)}) copy-start(bf16[2,1024,4,64]{1,3,2,0:T(8,128)(2,1)S(1)} %add_convert_fusion.3) | copy-start | bytes 3145732
  119.5 2.5 copy-start.30
  121.0 1.0 copy-start.18
  126.5 71.9 %copy-start.5 = (bf16[512,1024]{1,0:T(8,128)(2,1)S(1)}, bf16[512,1024]{1,0:T(8,128)(2,1)}, u32[]{:S(2)}) copy-start(bf16[512,1024]{1,0:T(8,128)(2,1)} %param.27) | copy-start | bytes 3145732
  126.5 71.9 %copy-start.43 = (f32[1024]{0:T(1024)S(1)}, f32[1024]{0:T(1024)}, u32[]{:S(2)}) copy-start(f32[1024]{0:T(1024)} %param.34) | copy-start | bytes 12292
  126.6 75.1 %copy-start.35 = (f32[1024]{0:T(1024)S(1)}, f32[1024]{0:T(1024)}, u32[]{:S(2)}) copy-start(f32[1024]{0:T(1024)} %param.35) | copy-start | bytes 12292
  126.6 75.1 %copy-start.41 = (f32[1024]{0:T(1024)S(1)}, f32[1024]{0:T(1024)}, u32[]{:S(2)}) copy-start(f32[1024]{0:T(1024)} %param.36) | copy-start | bytes 12292
  126.6 111.2 %all-gather.7.cloned.1.call-start = ((), (), s32[]{:S(2)}) async-start(), calls=%async_computation.6 | async-start | bytes 5242880 | tf_op jit(solution)/shard_map/all_gather | solution.py:121
  200.4 1.3 copy-start.3
  203.1 70.7 %all-gather.9.cloned.1.call-start = ((), (), s32[]{:S(2)}) async-start(), calls=%async_computation.8 | async-start | bytes 5242880 | tf_op jit(solution)/shard_map/all_gather | solution.py:136
  203.7 70.1 %copy-start.48 = (f32[1024]{0:T(1024)S(1)}, f32[1024]{0:T(1024)}, u32[]{:S(2)}) copy-start(f32[1024]{0:T(1024)} %param.38) | copy-start | bytes 12292
  203.7 163.7 %reduce-scatter.9.cloned.1.call-start = ((), (), s32[]{:S(2)}) async-start(), calls=%async_computation.9 | async-start | bytes 10485760 | tf_op jit(solution)/shard_map/reduce_scatter | solution.py:145
  273.8 14.8 %copy-start.47 = (bf16[1024,1024]{1,0:T(8,128)(2,1)S(1)}, bf16[1024,1024]{1,0:T(8,128)(2,1)}, u32[]{:S(2)}) copy-start(bf16[1024,1024]{1,0:T(8,128)(2,1)} %param.37) | copy-start | bytes 6291460
  286.6 2.0 copy-start.49
  295.5 119.4 %reduce-scatter.7.cloned.1.call-start = ((), (), s32[]{:S(2)}) async-start(), calls=%async_computation.7 | async-start | bytes 5242880 | tf_op jit(solution)/shard_map/reduce_scatter | solution.py:126
  307.4 60.0 %copy-start.4 = (f32[512,1024]{1,0:T(8,128)S(1)}, f32[512,1024]{1,0:T(8,128)}, u32[]{:S(2)}) copy-start(f32[512,1024]{1,0:T(8,128)} %copy-done.3) | copy-start | bytes 6291460
  307.4 107.5 %copy-start.42 = (f32[1024]{0:T(1024)S(1)}, f32[1024]{0:T(1024)}, u32[]{:S(2)}) copy-start(f32[1024]{0:T(1024)} %param.40) | copy-start | bytes 12292
  307.5 148.5 %all-gather.11.cloned.1.call-start = ((), (), s32[]{:S(2)}) async-start(), calls=%async_computation.10 | async-start | bytes 5242880 | tf_op jit(solution)/shard_map/all_gather | solution.py:153
  369.7 50.2 %copy-start.11 = (bf16[512,1024]{1,0:T(8,128)(2,1)S(1)}, bf16[512,1024]{1,0:T(8,128)(2,1)}, u32[]{:S(2)}) copy-start(bf16[512,1024]{1,0:T(8,128)(2,1)} %param.41) | copy-start | bytes 3145732
  418.6 1.3 copy-start.7
  418.6 37.4 %copy-start.31 = (bf16[256,1024]{1,0:T(8,128)(2,1)S(1)}, bf16[256,1024]{1,0:T(8,128)(2,1)}, u32[]{:S(2)}) copy-start(bf16[256,1024]{1,0:T(8,128)(2,1)} %param.33) | copy-start | bytes 1572868
  421.3 191.2 %reduce-scatter.11.cloned.1.call-start = ((), (), s32[]{:S(2)}) async-start(), calls=%async_computation.11 | async-start | bytes 5242880 | tf_op jit(solution)/shard_map/reduce_scatter | solution.py:210
  467.7 5.9 copy-start.17
  467.7 10.5 %slice-start = ((s8[8388608]{0:T(1024)(128)(4,1)}), s8[4194304]{0:T(1024)(128)(4,1)S(1)}, s32[]{:S(2)}) async-start(s8[8388608]{0:T(1024)(128)(4,1)} %bitcast.85), calls=%async_computation.13 | async-start | bytes 8388608
  473.6 4.6 slice-start.1
  478.3 2.5 copy-start.9
  480.7 1.6 copy-start.15
  487.0 11.6 %copy-start.20 = (bf16[2,512,4,64]{1,3,2,0:T(8,128)(2,1)S(1)}, bf16[2,512,4,64]{1,3,2,0:T(8,128)(2,1)}, u32[]{:S(2)}) copy-start(bf16[2,512,4,64]{1,3,2,0:T(8,128)(2,1)} %copy.87) | copy-start | bytes 1572868
  487.0 11.6 %copy-start.21 = (f32[2,512,4,64]{1,3,2,0:T(8,128)S(1)}, f32[2,512,4,64]{1,3,2,0:T(8,128)}, u32[]{:S(2)}) copy-start(f32[2,512,4,64]{1,3,2,0:T(8,128)} %fusion.38) | copy-start | bytes 3145732
  527.4 2.7 copy-start.25
  530.1 2.6 copy-start.27
  543.9 4.1 copy-start.28
  546.3 1.7 copy-start.10
  553.0 452.2 %all-reduce.7.cloned.1.call-start = ((), (), s32[]{:S(2)}) async-start(), calls=%async_computation.12 | async-start | bytes 25165824 | tf_op jit(solution)/shard_map/psum | solution.py:219
  553.3 10.1 copy-start.46
  575.1 5.0 copy-start.19
  580.1 4.6 copy-start.26
  580.1 4.6 copy-start.45
  589.9 22.6 %copy-start.6 = (bf16[512,1024]{1,0:T(8,128)(2,1)S(1)}, bf16[512,1024]{1,0:T(8,128)(2,1)}, u32[]{:S(2)}) copy-start(bf16[512,1024]{1,0:T(8,128)(2,1)} %param.27) | copy-start | bytes 3145732
  589.9 22.6 %copy-start.33 = (f32[512]{0:T(512)S(1)}, f32[512]{0:T(512)}, u32[]{:S(2)}) copy-start(f32[512]{0:T(512)} %copy-done.32) | copy-start | bytes 6148
  589.9 22.6 %copy-start.34 = (f32[1024]{0:T(1024)S(1)}, f32[1024]{0:T(1024)}, u32[]{:S(2)}) copy-start(f32[1024]{0:T(1024)} %param.29) | copy-start | bytes 12292
  589.9 24.6 %copy-start.40 = (f32[512]{0:T(512)S(1)}, f32[512]{0:T(512)}, u32[]{:S(2)}) copy-start(f32[512]{0:T(512)} %copy-done.39) | copy-start | bytes 6148
  589.9 24.6 %copy-start.38 = (f32[512]{0:T(512)S(1)}, f32[512]{0:T(512)}, u32[]{:S(2)}) copy-start(f32[512]{0:T(512)} %copy-done.37) | copy-start | bytes 6148
  612.5 4.5 copy-start.12
  1005.2 3.9 copy-start.29
  1005.2 4.9 copy-start.24
  1010.1 3.7 copy-start.23
  1010.1 5.7 copy-start.1
Sparse Core Ops, SparseCore 0:
  14.5 37.1 all-gather.4
  126.7 71.7 reduce-scatter.4
  203.2 34.4 all-gather.6
  239.2 34.4 all-gather.8
  295.6 71.6 reduce-scatter.8
  370.3 44.4 reduce-scatter.6
  421.4 34.4 all-gather.10
  553.1 44.4 reduce-scatter.10
  603.6 401.5 all-reduce.6
where the time goes:
time: 1030 us; the launch traced here: 1020 us
  waiting for transfers between devices  644 us (63%)
  matrix products  153 us (15%)
  local copies, waits for them, and re-layouts  83.2 us (8%)
  blocking collectives  64.8 us (6%)
  other arithmetic  62.2 us (6%)
  between operations  14.9 us (1%)
    psum x1, waiting for transfers between devices, body(): lax.psum((qkv_grad, qv_bias_grad, mix_grad, expand_grad, expand_bias_grad...  343 us
    reduce_scatter x1, waiting for transfers between devices, body(): lax.psum_scatter(jnp.dot(rows_part, w_mix, preferred_element_type=jnp.flo...  71.8 us
    reduce_scatter x1, waiting for transfers between devices, body(): lax.psum_scatter(times_transpose(rows_part, w_expand), 'tensor', scatter_...  59.9 us
    reduce_scatter x1, waiting for transfers between devices, body(): lax.psum_scatter(jnp.dot(rows_part, w_reduce, preferred_element_type=jnp....  45.1 us
    psum x1, blocking collectives, body(): lax.psum((first_gain_grad, first_shift_grad, mix_bias_grad, second_gain_g...  42.3 us
    all_gather x1, waiting for transfers between devices, body(): mixed_rows = lax.all_gather(mixed_grad, 'tensor', axis=0, tiled=True)  34.5 us
    all_gather x1, waiting for transfers between devices, body(): rows_two = lax.all_gather(normed_two, 'tensor', axis=0, tiled=True)  33.8 us
    dot_general x4, matrix products, contract_rows(): lax.dot_general(left_mat, right_mat, (((0,), (0,)), ((), ())), preferred_...  31.6 us
  transfers between devices with their start and end apart: 9, of which 8 were waited for; matrix products, arithmetic and copies ran while one was open for 7% of the time, Pallas kernels for 0%

commit v1 on v0

v1 whole, which is shorter than its diff:
```python
import functools

import jax
import jax.numpy as jnp
from jax import lax
from jax.experimental import pallas as pl
from jax.experimental.pallas import tpu as pltpu
from jax.sharding import PartitionSpec as P

HD = 64
PAIR = 2 * HD
QB = 256
EPS = 1e-5
BF = jnp.bfloat16
F32 = jnp.float32
SCALE = HD ** (-0.5)
NT = (((1,), (1,)), ((), ()))
TN = (((0,), (0,)), ((), ()))


def dot(a, b, dims=(((1,), (0,)), ((), ()))):
    return lax.dot_general(a, b, dims, preferred_element_type=F32)


def after(a, other):
    return lax.optimization_barrier((a, other))[0]


def swap(a, bit):
    return lax.ppermute(a, "tensor", [(i, i ^ bit) for i in range(4)])


def fill_bias(segc_ref, segr_ref, bias_ref, blocks):
    off = 0
    for i in range(blocks):
        keys = (i + 1) * QB
        kpos = lax.broadcasted_iota(jnp.int32, (keys, QB), 0)
        qpos = lax.broadcasted_iota(jnp.int32, (keys, QB), 1) + i * QB
        same = segc_ref[:keys, :] == segr_ref[:, i * QB : (i + 1) * QB]
        allowed = jnp.logical_and(kpos <= qpos, same)
        bias_ref[off : off + keys, :] = jnp.where(allowed, 0.0, -1e30)
        off += keys


def half_masks():
    lane = lax.broadcasted_iota(jnp.int32, (1, PAIR), 1)
    return (lane < HD, lane >= HD)


def attn_fwd_kernel(blocks, segc_ref, segr_ref, q_ref, k_ref, v_ref, o_ref, bias_ref):
    @pl.when(pl.program_id(0) == 0)
    def _():
        fill_bias(segc_ref, segr_ref, bias_ref, blocks)

    masks = half_masks()
    vt = v_ref[...].T
    off = 0
    for i in range(blocks):
        keys = (i + 1) * QB
        qi = q_ref[i * QB : (i + 1) * QB, :] * jnp.asarray(SCALE, BF)
        outs = []
        for h in range(2):
            qm = jnp.where(masks[h], qi, jnp.zeros_like(qi))
            s = dot(k_ref[:keys, :], qm, NT) + bias_ref[off : off + keys, :]
            e = jnp.exp(s - jnp.max(s, axis=0, keepdims=True))
            total = jnp.sum(e, axis=0, keepdims=True)
            o = dot(vt[h * HD : (h + 1) * HD, :keys], e.astype(BF))
            outs.append(o * (1.0 / total))
        o_ref[i * QB : (i + 1) * QB, :] = jnp.concatenate(outs, axis=0).T.astype(BF)
        off += keys


def attn_fwd(qkv, segc, segr):
    rows, cols = qkv.shape
    pairs = cols // 3 // PAIR
    blocks = rows // QB

    def col(base):
        return pl.BlockSpec((rows, PAIR), lambda p: (0, base * pairs + p))

    return pl.pallas_call(
        functools.partial(attn_fwd_kernel, blocks),
        grid=(pairs,),
        in_specs=[
            pl.BlockSpec((rows, 1), lambda p: (0, 0)),
            pl.BlockSpec((1, rows), lambda p: (0, 0)),
            col(0),
            col(1),
            col(2),
        ],
        out_specs=pl.BlockSpec((rows, PAIR), lambda p: (0, p)),
        out_shape=jax.ShapeDtypeStruct((rows, cols // 3), BF),
        scratch_shapes=[pltpu.VMEM((QB * blocks * (blocks + 1) // 2, QB), F32)],
        compiler_params=pltpu.CompilerParams(vmem_limit_bytes=48 << 20),
        cost_estimate=pl.CostEstimate(
            flops=8 * pairs * rows * rows * HD,
            bytes_accessed=qkv.size * 4,
            transcendentals=pairs * rows * rows,
        ),
        name="attn_fwd",
    )(segc, segr, qkv, qkv, qkv)


def attn_bwd_kernel(
    blocks, pairs, segc_ref, segr_ref, q_ref, k_ref, v_ref, g_ref, d_ref, sum_ref, bias_ref, dk_ref, dv_ref
):
    p_id = pl.program_id(0)

    @pl.when(p_id == 0)
    def _():
        fill_bias(segc_ref, segr_ref, bias_ref, blocks)

    def place(base):
        return pl.ds(pl.multiple_of((base * pairs + p_id) * PAIR, PAIR), PAIR)

    masks = half_masks()
    kt = k_ref[...].T
    dk_ref[...] = jnp.zeros_like(dk_ref)
    dv_ref[...] = jnp.zeros_like(dv_ref)
    off = 0
    qsum = jnp.zeros((1, PAIR), F32)
    for i in range(blocks):
        keys = (i + 1) * QB
        rows = slice(i * QB, (i + 1) * QB)
        qi = q_ref[rows, :] * jnp.asarray(SCALE, BF)
        gi = g_ref[rows, :]
        outs = []
        for h in range(2):
            qm = jnp.where(masks[h], qi, jnp.zeros_like(qi))
            gm = jnp.where(masks[h], gi, jnp.zeros_like(gi))
            s = dot(k_ref[:keys, :], qm, NT) + bias_ref[off : off + keys, :]
            e = jnp.exp(s - jnp.max(s, axis=0, keepdims=True))
            prob = e * (1.0 / jnp.sum(e, axis=0, keepdims=True))
            weighted = prob * dot(v_ref[:keys, :], gm, NT)
            ds = (weighted - prob * jnp.sum(weighted, axis=0, keepdims=True)).astype(BF)
            dv_ref[:keys, :] += dot(prob.astype(BF), gm)
            dk_ref[:keys, :] += dot(ds, qm)
            outs.append(dot(kt[h * HD : (h + 1) * HD, :keys], ds))
        dq = (jnp.concatenate(outs, axis=0).T * SCALE).astype(BF)
        d_ref[rows, place(0)] = dq
        qsum += jnp.sum(dq.astype(F32), axis=0, keepdims=True)
        off += keys
    dv = dv_ref[...].astype(BF)
    d_ref[:, place(1)] = dk_ref[...].astype(BF)
    d_ref[:, place(2)] = dv
    at = pl.ds(pl.multiple_of(p_id * PAIR, PAIR), PAIR)
    sum_ref[0:1, at] = qsum
    sum_ref[1:2, at] = jnp.sum(dv.astype(F32), axis=0, keepdims=True)


def attn_bwd(qkv, grad, segc, segr):
    rows, cols = qkv.shape
    pairs = cols // 3 // PAIR
    blocks = rows // QB

    def col(base):
        return pl.BlockSpec((rows, PAIR), lambda p: (0, base * pairs + p))

    return pl.pallas_call(
        functools.partial(attn_bwd_kernel, blocks, pairs),
        grid=(pairs,),
        in_specs=[
            pl.BlockSpec((rows, 1), lambda p: (0, 0)),
            pl.BlockSpec((1, rows), lambda p: (0, 0)),
            col(0),
            col(1),
            col(2),
            col(0),
        ],
        out_specs=[
            pl.BlockSpec((rows, cols), lambda p: (0, 0)),
            pl.BlockSpec((2, cols // 3), lambda p: (0, 0)),
        ],
        out_shape=[
            jax.ShapeDtypeStruct((rows, cols), BF),
            jax.ShapeDtypeStruct((2, cols // 3), F32),
        ],
        scratch_shapes=[
            pltpu.VMEM((QB * blocks * (blocks + 1) // 2, QB), F32),
            pltpu.VMEM((rows, PAIR), F32),
            pltpu.VMEM((rows, PAIR), F32),
        ],
        compiler_params=pltpu.CompilerParams(vmem_limit_bytes=48 << 20),
        cost_estimate=pl.CostEstimate(
            flops=24 * pairs * rows * rows * HD,
            bytes_accessed=qkv.size * 6,
            transcendentals=pairs * rows * rows,
        ),
        name="attn_bwd",
    )(segc, segr, qkv, qkv, qkv, grad)


GA = 0.7978845608028654
GB = 0.044715


def ff_kernel(
    half, n_a, n_b, g_a, g_b, we_ref, wr_ref, be_ref, _act, _pg, act_ref, pg_ref, branch_ref, ng_ref, sum_ref
):
    i = pl.program_id(0)
    first = i < half
    rows = jnp.where(first, n_a[...], n_b[...])
    grads = jnp.where(first, g_a[...], g_b[...])
    u = dot(rows, we_ref[...]) + be_ref[...]
    act_grad = dot(grads, wr_ref[...], NT)
    sq = u * u
    th = jnp.tanh(u * (GA + (GA * GB) * sq))
    cdf = 0.5 * (1.0 + th)
    act = (u * cdf).astype(BF)
    slope = cdf + (0.5 * u) * (1.0 - th * th) * (GA + (3.0 * GA * GB) * sq)
    pre = (act_grad * slope).astype(BF)
    act_ref[...] = act
    pg_ref[...] = pre
    branch_ref[...] = dot(act, wr_ref[...]).astype(BF)
    ng_ref[...] = dot(pre, we_ref[...], NT).astype(BF)

    @pl.when(i == 0)
    def _():
        sum_ref[...] = jnp.zeros_like(sum_ref)

    sum_ref[...] += jnp.sum(pre.astype(F32), axis=0, keepdims=True)


def ff_part(part, n_a, n_b, g_a, g_b, we, wr, be, act, pg):
    rows, width = n_a.shape
    units = we.shape[1]
    block = 256
    half = rows // block
    base = 2 * half * part

    def lo():
        return pl.BlockSpec((block, width), lambda i: (jnp.minimum(i, half - 1), 0))

    def hi():
        return pl.BlockSpec((block, width), lambda i: (jnp.maximum(i - half, 0), 0))

    def whole(a):
        return pl.BlockSpec(a.shape, lambda i: (0, 0), pipeline_mode=pl.Buffered(1))

    here = pl.BlockSpec((block, units), lambda i: (i + base, 0))
    out = pl.BlockSpec((block, width), lambda i: (i, 0))
    return pl.pallas_call(
        functools.partial(ff_kernel, half),
        grid=(2 * half,),
        in_specs=[
            lo(),
            hi(),
            lo(),
            hi(),
            whole(we),
            whole(wr),
            whole(be),
            pl.BlockSpec(memory_space=pl.ANY),
            pl.BlockSpec(memory_space=pl.ANY),
        ],
        out_specs=[here, here, out, out, pl.BlockSpec((1, units), lambda i: (0, 0))],
        out_shape=[
            jax.ShapeDtypeStruct(act.shape, BF),
            jax.ShapeDtypeStruct(pg.shape, BF),
            jax.ShapeDtypeStruct((2 * rows, width), BF),
            jax.ShapeDtypeStruct((2 * rows, width), BF),
            jax.ShapeDtypeStruct((1, units), F32),
        ],
        input_output_aliases={7: 0, 8: 1},
        compiler_params=pltpu.CompilerParams(vmem_limit_bytes=52 << 20),
        cost_estimate=pl.CostEstimate(
            flops=16 * rows * width * units,
            bytes_accessed=4 * width * units + 20 * rows * width,
            transcendentals=2 * rows * units,
        ),
        name="ff_part",
    )(n_a, n_b, g_a, g_b, we, wr, be, act, pg)


MESH_ID = pl.DeviceIdType.MESH


def ring_kernel(
    n, x_ref, small_ref, r_ref, e_ref, xo_ref, so_ref, ro_ref, eo_ref, xbuf, sbuf, send, recv, local
):
    half = n // 2
    mine = lax.axis_index("dp")
    odd = mine % 2
    pos = (1 - odd) * (mine // 2) + odd * (n - 1 - mine // 2)

    def index_of(at):
        at = (at + 2 * n) % n
        far = at // half
        return (1 - far) * 2 * at + far * (2 * (n - 1 - at) + 1)

    sides = (index_of(pos + 1), index_of(pos - 1))
    barrier = pltpu.get_barrier_semaphore()
    for side in sides:
        pl.semaphore_signal(barrier, inc=1, device_id={"dp": side}, device_id_type=MESH_ID)
    pl.semaphore_wait(barrier, 2)

    def remote(src, dst, kind, d, s):
        return pltpu.make_async_remote_copy(
            src_ref=src,
            dst_ref=dst,
            send_sem=send.at[kind, d],
            recv_sem=recv.at[kind, d, s],
            device_id={"dp": sides[d]},
            device_id_type=MESH_ID,
        )

    def gather(out, kind, d, s):
        chunk = index_of(pos - s if d == 0 else pos + s)
        return remote(out.at[chunk, d], out.at[chunk, d], kind, d, s)

    def gather_small(s):
        chunk = index_of(pos - s)
        return remote(so_ref.at[chunk], so_ref.at[chunk], 5, 0, s)

    def part(d, s):
        return index_of(pos - 1 - s if d == 0 else pos + 1 + s)

    def reduce_first(d):
        return remote(x_ref.at[part(d, 0), d], xbuf.at[0, d], 0, d, 0)

    def reduce_next(d, s):
        return remote(xbuf.at[s - 1, d], xbuf.at[s, d], 0, d, s)

    def small_first():
        return remote(small_ref.at[part(0, 0)], sbuf.at[0], 4, 0, 0)

    def small_next(s):
        return remote(sbuf.at[s - 1], sbuf.at[s], 4, 0, s)

    def add(d, s):
        chunk = part(d, s + 1)
        xbuf[s, d] = (xbuf[s, d].astype(F32) + x_ref[chunk, d].astype(F32)).astype(BF)

    def add_small(s):
        sbuf[s] = sbuf[s] + small_ref[part(0, s + 1)]

    own_r = pltpu.make_async_copy(r_ref, ro_ref.at[mine], local.at[0])
    own_e = pltpu.make_async_copy(e_ref, eo_ref.at[mine], local.at[1])
    own_r.start()
    own_e.start()
    for d in range(2):
        reduce_first(d).start()
    small_first().start()
    own_r.wait()
    own_e.wait()
    for d in range(2):
        gather(ro_ref, 1, d, 0).start()

    @pl.loop(1, n - 1)
    def _(s):
        for d in range(2):
            reduce_first(d).wait_send()
            remote(xbuf.at[s - 1, d], xbuf.at[s - 1, d], 0, d, s - 1).wait_recv()
            add(d, s - 1)
            reduce_next(d, s).start()
        small_first().wait_send()
        remote(sbuf.at[s - 1], sbuf.at[s - 1], 4, 0, s - 1).wait_recv()
        add_small(s - 1)
        small_next(s).start()
        for d in range(2):
            gather(ro_ref, 1, d, s - 1).wait()
            gather(ro_ref, 1, d, s).start()

    last = n - 2
    for d in range(2):
        reduce_first(d).wait_send()
        remote(xbuf.at[last, d], xbuf.at[last, d], 0, d, last).wait_recv()
        add(d, last)
    small_first().wait_send()
    remote(sbuf.at[last], sbuf.at[last], 4, 0, last).wait_recv()
    add_small(last)
    own_x = pltpu.make_async_copy(xbuf.at[last], xo_ref.at[mine], local.at[0])
    own_s = pltpu.make_async_copy(sbuf.at[last], so_ref.at[mine], local.at[1])
    own_x.start()
    own_s.start()
    for d in range(2):
        gather(ro_ref, 1, d, last).wait()
        gather(eo_ref, 2, d, 0).start()
    own_x.wait()
    own_s.wait()
    for d in range(2):
        gather(xo_ref, 3, d, 0).start()
    gather_small(0).start()

    @pl.loop(1, n - 1)
    def _(s):
        for d in range(2):
            gather(eo_ref, 2, d, s - 1).wait()
            gather(eo_ref, 2, d, s).start()
        for d in range(2):
            gather(xo_ref, 3, d, s - 1).wait()
            gather(xo_ref, 3, d, s).start()
        gather_small(s - 1).wait()
        gather_small(s).start()

    for d in range(2):
        gather(eo_ref, 2, d, last).wait()
        gather(xo_ref, 3, d, last).wait()
    gather_small(last).wait()


def ring_sum(x, small, r_own, e_own, n):
    rows, width = x.shape
    h = rows // (2 * n)
    m = small.size // n
    full = jax.ShapeDtypeStruct((n, 2, h, width), BF)
    vmem = pl.BlockSpec(memory_space=pltpu.VMEM)
    anyspace = pl.BlockSpec(memory_space=pl.ANY)
    xo, so, ro, eo = pl.pallas_call(
        functools.partial(ring_kernel, n),
        in_specs=[vmem, vmem, anyspace, anyspace],
        out_specs=[anyspace] * 4,
        out_shape=[full, jax.ShapeDtypeStruct((n, 1, m), F32), full, full],
        scratch_shapes=[
            pltpu.VMEM((n - 1, 2, h, width), BF),
            pltpu.VMEM((n - 1, 1, m), F32),
            pltpu.SemaphoreType.DMA((6, 2)),
            pltpu.SemaphoreType.DMA((6, 2, n - 1)),
            pltpu.SemaphoreType.DMA((2,)),
        ],
        compiler_params=pltpu.CompilerParams(
            collective_id=1, has_side_effects=True, vmem_limit_bytes=32 << 20
        ),
        name="ring_sum",
    )(
        x.reshape(n, 2, h, width),
        small.reshape(n, 1, m),
        r_own.reshape(2, h, width),
        e_own.reshape(2, h, width),
    )
    flat = (rows, width)
    return xo.reshape(flat), so.reshape(small.shape), ro.reshape(flat), eo.reshape(flat)


def norm_stats(values):
    mean = jnp.mean(values, axis=-1, keepdims=True)
    centered = values - mean
    variance = jnp.mean(centered * centered, axis=-1, keepdims=True)
    scale = lax.rsqrt(variance + EPS)
    return centered * scale, scale


def norm_back(grad, gain, normed, scale):
    g = grad * gain
    inner = g - jnp.mean(g, axis=-1, keepdims=True)
    inner = inner - normed * jnp.mean(g * normed, axis=-1, keepdims=True)
    return scale * inner, jnp.sum(grad * normed, axis=0), jnp.sum(grad, axis=0)


def body(
    block_in,
    segments,
    first_gain,
    first_shift,
    w_qkv,
    qv_bias,
    w_mix,
    mix_bias,
    second_gain,
    second_shift,
    w_expand,
    expand_bias,
    w_reduce,
    reduce_bias,
    out_grad,
):
    rows, width = block_in.shape
    cols = w_qkv.shape[2]
    units = w_expand.shape[1]
    place = lax.axis_index("tensor")
    core = place % 2
    seg = lax.dynamic_slice_in_dim(segments, place // 2, 1, 0)
    segc = seg.reshape(-1, 1)

    def in_order(own, other):
        return jnp.where(
            core == 0,
            jnp.concatenate([own, other], axis=0),
            jnp.concatenate([other, own], axis=0),
        )

    def own_rows(a):
        return lax.dynamic_slice_in_dim(a, core * rows, rows, 0)

    def other_rows(a):
        return lax.dynamic_slice_in_dim(a, (1 - core) * rows, rows, 0)

    dp_size = lax.axis_size("dp")
    dp_place = lax.axis_index("dp")

    wq = w_qkv.reshape(width, 3 * cols)
    top = width // 2
    mid = cols // 2
    near_half = jnp.concatenate([wq[:top], w_mix[:mid].reshape(top, cols)], axis=1)
    slice_rows = top // dp_size
    far_half = jnp.concatenate(
        [
            lax.dynamic_slice_in_dim(wq, top + dp_place * slice_rows, slice_rows, 0),
            lax.dynamic_slice_in_dim(
                w_mix[mid:].reshape(top, cols), dp_place * slice_rows, slice_rows, 0
            ),
        ],
        axis=1,
    )
    piece = swap(far_half, 2)
    low = lax.all_gather(piece, "dp", axis=0, tiled=True)
    near_half = after(near_half, piece)
    high = swap(near_half, 2)
    qb_far = swap(qv_bias, 2)
    wq_far = jnp.concatenate([high[:, : 3 * cols], low[:, : 3 * cols]], axis=0)
    wm_far = jnp.concatenate(
        [high[:, 3 * cols :].reshape(mid, width), low[:, 3 * cols :].reshape(mid, width)], axis=0
    )

    x = block_in.astype(F32)
    norm1, scale1 = norm_stats(x)
    n1 = (norm1 * first_gain + first_shift).astype(BF)
    rows1 = in_order(n1, swap(n1, 1))

    def project(w, b):
        bias = jnp.concatenate([b[0], jnp.zeros_like(b[0]), b[1]])
        return (dot(rows1, w) + bias).astype(BF)

    qkv_a = project(wq, qv_bias)
    att_a = attn_fwd(qkv_a, segc, seg)
    wq_far, att_a, wm_far = lax.optimization_barrier((wq_far, att_a, wm_far))
    qkv_b = project(wq_far, qb_far)
    att_b = attn_fwd(qkv_b, segc, seg)

    part = dot(other_rows(att_a), w_mix) + dot(other_rows(att_b), wm_far)
    got = swap(part.astype(BF), 1)
    mixed = dot(own_rows(att_a), w_mix) + dot(own_rows(att_b), wm_far) + got.astype(F32) + mix_bias
    resid = x + mixed
    norm2, scale2 = norm_stats(resid)
    n2 = (norm2 * second_gain + second_shift).astype(BF)

    og_s = swap(out_grad, 1)
    og_y = swap(after(out_grad, high), 2)
    og_d = swap(og_y, 1)

    n2_y = swap(n2, 2)
    n2_s = swap(n2, 1)

    be = expand_bias.reshape(1, units)
    act = jnp.zeros((4 * rows, units), BF)
    pg = jnp.zeros((4 * rows, units), BF)
    act, pg, br0, ng0, sum0 = ff_part(0, n2, n2_s, out_grad, og_s, w_expand, w_reduce, be, act, pg)
    n2_y, og_y, og_d, act = lax.optimization_barrier((n2_y, og_y, og_d, act))
    n2_d = swap(n2_y, 1)
    act, pg, br1, ng1, sum1 = ff_part(1, n2_y, n2_d, og_y, og_d, w_expand, w_reduce, be, act, pg)

    def across(far):
        return (far[:rows].astype(F32) + swap(far[rows:], 1).astype(F32)).astype(BF)

    def near_sum(near):
        return near[:rows].astype(F32) + swap(near[rows:], 1).astype(F32)

    ng_got = swap(across(ng1), 2)
    br_got = swap(after(across(br1), ng_got), 2)

    grads_all = jnp.concatenate([out_grad, og_s, og_y, og_d], axis=0)
    n2_all = jnp.concatenate([n2, n2_s, n2_y, n2_d], axis=0)
    reduce_grad = dot(act, grads_all, TN).astype(BF)
    reduce_own = lax.psum_scatter(reduce_grad, "dp", scatter_dimension=0, tiled=True)
    expand_grad = dot(n2_all, pg, TN).astype(BF)
    expand_own = lax.psum_scatter(expand_grad, "dp", scatter_dimension=0, tiled=True)
    expand_bias_grad = (sum0 + sum1)[0]

    ng_got, reduce_grad, expand_grad = lax.optimization_barrier((ng_got, reduce_grad, expand_grad))
    ng = near_sum(ng0) + ng_got.astype(F32)
    grad = out_grad.astype(F32)
    reduce_bias_grad = jnp.sum(grad, axis=0)
    back2, second_gain_grad, second_shift_grad = norm_back(ng, second_gain, norm2, scale2)
    resid_grad = grad + back2
    mg = resid_grad.astype(BF)
    mix_bias_grad = jnp.sum(mg.astype(F32), axis=0)

    mg_all = in_order(mg, swap(mg, 1))
    ag_b = dot(mg_all, wm_far, NT).astype(BF)
    dqkv_b, sums_b = attn_bwd(qkv_b, ag_b, segc, seg)
    qkv_grad_b = dot(rows1, dqkv_b, TN).astype(BF)
    mix_grad_b = dot(att_b, mg_all, TN).astype(BF)
    mix_back = swap(mix_grad_b, 2)
    qkv_back = swap(qkv_grad_b, 2)
    sums_back = swap(sums_b, 2)
    ag_a = dot(after(mg_all, qkv_grad_b), w_mix, NT).astype(BF)
    dqkv_a, sums_a = attn_bwd(qkv_a, ag_a, segc, seg)
    qkv_back, mix_back, dqkv_a, br_got = lax.optimization_barrier((qkv_back, mix_back, dqkv_a, br_got))

    branch = near_sum(br0) + br_got.astype(F32)
    block_out = (resid + branch + reduce_bias).astype(BF)

    n1g_other = dot(other_rows(dqkv_b), wq_far, NT) + dot(other_rows(dqkv_a), wq, NT)
    n1g_got = swap(n1g_other.astype(BF), 1)
    n1g = dot(own_rows(dqkv_b), wq_far, NT) + dot(own_rows(dqkv_a), wq, NT) + n1g_got.astype(F32)
    back1, first_gain_grad, first_shift_grad = norm_back(n1g, first_gain, norm1, scale1)
    in_grad = resid_grad + back1

    def over_tensor(parts):
        a = jnp.stack(parts)
        a = a + swap(a, 1)
        return a + swap(a, 2)

    early = over_tensor([mix_bias_grad, second_gain_grad, second_shift_grad, reduce_bias_grad])
    late = over_tensor([first_gain_grad, first_shift_grad])

    mix_grad = (dot(att_a, mg_all, TN) + mix_back.astype(F32)).astype(BF)
    qkv_grad = (dot(rows1, dqkv_a, TN) + qkv_back.astype(F32)).astype(BF)
    packed = jnp.concatenate([qkv_grad, mix_grad.reshape(width, cols)], axis=1)
    qv_bias_grad = (sums_a + sums_back).reshape(1, 2 * cols)
    small = jnp.concatenate(
        [
            late,
            early,
            expand_bias_grad.reshape(1, units),
            jnp.pad(qv_bias_grad, ((0, 0), (0, width - 2 * cols))),
        ],
        axis=0,
    )
    packed, small, reduce_all, expand_all = ring_sum(packed, small, reduce_own, expand_own, dp_size)
    return (
        block_out,
        in_grad,
        small[0],
        small[1],
        packed[:, : 3 * cols].astype(F32).reshape(width, 3, cols),
        small[7, : 2 * cols].reshape(2, cols),
        packed[:, 3 * cols :].astype(F32).reshape(cols, width),
        small[2],
        small[3],
        small[4],
        expand_all.astype(F32),
        small[6],
        reduce_all.astype(F32),
        small[5],
    )


def solution(mesh):
    both = P(("dp", "tensor"), None)
    return jax.shard_map(
        body,
        mesh=mesh,
        in_specs=(
            both,
            P("dp", None),
            P(),
            P(),
            P(None, None, "tensor"),
            P(None, "tensor"),
            P("tensor", None),
            P(),
            P(),
            P(),
            P(None, "tensor"),
            P("tensor"),
            P("tensor", None),
            P(),
            both,
        ),
        out_specs=(
            both,
            both,
            P(),
            P(),
            P(None, None, "tensor"),
            P(None, "tensor"),
            P("tensor", None),
            P(),
            P(),
            P(),
            P(None, "tensor"),
            P("tensor"),
            P("tensor", None),
            P(),
        ),
        check_vma=False,
    )
```

time: 1030 us -> 420 us (0.41)
  waiting for transfers between devices: 644 us -> 94.1 us
  Pallas kernels: 0 us -> 159 us
  matrix products: 153 us -> 52.4 us
  blocking collectives: 64.8 us -> 0 us
  local copies, waits for them, and re-layouts: 83.2 us -> 40.4 us
  other arithmetic: 62.2 us -> 34.7 us
  starting transfers between devices: 0.97 us -> 19.6 us
    psum x1 -> x0, waiting for transfers between devices: 343 us -> none  [body(): lax.psum((qkv_grad, qv_bias_grad, mix_grad, expand_grad, expand_bias_grad...]
    reduce_scatter x4 -> x2, waiting for transfers between devices: 177 us -> 0.04 us  [the longest x1 0.02 us: body(): lax.psum_scatter(expand_grad, 'dp', scatter_dimension=0, tiled=True)]
    pallas_call x0 -> x7, Pallas kernels: none -> 159 us  [the longest x1 84.1 us: ring_sum(): pl.pallas_call(functools.partial(ring_kernel, n), in_specs=[vmem, vmem, a...]
    all_gather x4 -> x1, waiting for transfers between devices: 124 us -> 10.4 us  [body(): low = lax.all_gather(piece, 'dp', axis=0, tiled=True)]
    dot_general x24 -> x18, matrix products: 153 us -> 52.4 us  [dot(): return lax.dot_general(a, b, dims, preferred_element_type=F32)]
    ppermute x0 -> x26, waiting for transfers between devices: none -> 83.5 us  [swap(): return lax.ppermute(a, 'tensor', [(i, i ^ bit) for i in range(4)])]
    psum x2 -> x0, blocking collectives: 64.8 us -> none  [the longest x1 42.3 us: body(): lax.psum((first_gain_grad, first_shift_grad, mix_bias_grad, second_gain_g...]
    reduce_sum x13 -> x5, other arithmetic: 37 us -> 8.89 us  [the longest x1 4.27 us: body(): mix_bias_grad = jnp.sum(mg.astype(F32), axis=0)]
  transfers between devices with their start and end apart: 9 -> 29, of which waited for: 8 -> 11; matrix products, arithmetic and copies ran while one was open for 7% -> 20% of each run, Pallas kernels for 0% -> 12%
where the time goes in v1:
time: 420 us; the launch traced here: 416 us
  Pallas kernels  159 us (38%)
  waiting for transfers between devices  94.1 us (22%)
  matrix products  52.4 us (12%)
  local copies, waits for them, and re-layouts  40.4 us (10%)
  other arithmetic  34.7 us (8%)
  starting transfers between devices  19.6 us (5%)
  between operations  15.1 us (4%)
    pallas_call x1, Pallas kernels, ring_sum(): pl.pallas_call(functools.partial(ring_kernel, n), in_specs=[vmem, vmem, a...  84.1 us
    ppermute x26, waiting for transfers between devices, swap(): return lax.ppermute(a, 'tensor', [(i, i ^ bit) for i in range(4)])  83.5 us
    dot_general x18, matrix products, dot(): return lax.dot_general(a, b, dims, preferred_element_type=F32)  52.4 us
    pallas_call x2, Pallas kernels, ff_part(): pl.pallas_call(functools.partial(ff_kernel, half), grid=(2 * half,), in_s...  30 us
    pallas_call x2, Pallas kernels, attn_bwd(): pl.pallas_call(functools.partial(attn_bwd_kernel, blocks, pairs), grid=(p...  27.2 us
    ppermute x26, starting transfers between devices, swap(): return lax.ppermute(a, 'tensor', [(i, i ^ bit) for i in range(4)])  19.1 us
    pallas_call x2, Pallas kernels, attn_fwd(): pl.pallas_call(functools.partial(attn_fwd_kernel, blocks), grid=(pairs,),...  18.2 us
    unnamed x135, local copies, waits for them, and re-layouts  16.3 us
  transfers between devices with their start and end apart: 29, of which 11 were waited for; matrix products, arithmetic and copies ran while one was open for 20% of the time, Pallas kernels for 12%

profile of v1, /device:TPU:0, one launch (start us, length us, event | category | flops | bytes accessed | tf_op | source)
XLA Modules:
  0.0 415.7 jit_solution(9143523740497821981)
XLA Ops:
  7.3 1.8 copy.53
  9.8 1.4 reshape.155
  11.5 3.0 collective-permute-start
  15.2 5.7 %collective-permute-done = bf16[64,1024]{0,1:T(8,128)(2,1)S(1)} collective-permute-done((bf16[64,1024]{0,1:T(8,128)(2,1)S(1)}, bf16[64,1024]{0,1:T(8,128)(2,1)S(1)}, u32[]{:S(2)}, u32[]{:S(2)}) %collective-permute-start) | collective-permute-done | bytes 131104 | tf_op jit(solution)/shard_map/ppermute | solution.py:30
  21.7 1.4 fusion.23
  23.2 1.7 collective-permute-start.3
  27.0 4.6 %add_convert_fusion.2.q_ref.k_ref.v_ref = bf16[1024,768]{1,0:T(8,128)(2,1)S(1)} fusion(bf16[1024,768]{0,1:T(8,128)(2,1)} %bitcast.71, f32[768]{0:T(1024)S(1)} %get-tuple-element.150, bf16[512,1024]{1,0:T(8,128)(2,1)} %collective-permute-done.2, bf16[512,1024]{1,0:T(8,128)(2,1)} %fusion.23, pred[]{:T(512)S(6)} %eq.6), kind=kOutput, calls=%fused_computation.18 | convolution fusion | flops 1621622784 | bytes 5245953 | tf_op jit(solution)/shard_map/dot_general | solution.py:22
  31.7 9.1 %attn_fwd.2 = bf16[1024,256]{1,0:T(8,128)(2,1)S(1)} custom-call(s32[1024,1]{1,0:T(8,128)S(1)} %copy.59.segc_ref, s32[1,1024]{1,0:T(1,128)S(1)} %constant_dynamic-slice_fusion.segr_ref, bf16[1024,768]{1,0:T(8,128)(2,1)S(1)} %add_convert_fusion.2.q_ref.k_ref.v_ref, bf16[1024,768]{1,0:T(8,128)(2,1)S(1)} %add_convert_fusion.2.q_ref.k_ref.v_ref, ...), custom_call_target="tpu_custom_call" | custom-call | flops 1073741824 | bytes 3145728 | tf_op jit(solution)/shard_map/attn_fwd/pallas_call | solution.py:81
  41.5 10.3 %collective-permute-done.1 = bf16[512,1024]{0,1:T(8,128)(2,1)S(1)} collective-permute-done((bf16[512,1024]{0,1:T(8,128)(2,1)}, bf16[512,1024]{0,1:T(8,128)(2,1)S(1)}, u32[]{:S(2)}, u32[]{:S(2)}) %collective-permute-start.1) | collective-permute-done | bytes 1048608 | tf_op jit(solution)/shard_map/ppermute | solution.py:30
  52.9 10.4 %all-gather.2.cloned.1.call-done = bf16[512,1024]{1,0:T(8,128)(2,1)} async-done(((bf16[64,1024]{1,0:T(8,128)(2,1)}), bf16[512,1024]{1,0:T(8,128)(2,1)}) %all-gather.2.cloned.1.call-update) | async-done | bytes 1048592 | tf_op jit(solution)/shard_map/all_gather | solution.py:506
  63.4 1.7 slice.131
  65.1 1.8 reshape.158
  66.9 1.2 copy.68
  68.1 1.1 pad_maximum_fusion.3
  69.2 1.5 pad_maximum_fusion.1
  70.7 4.6 %add_convert_fusion.1.q_ref.k_ref.v_ref = bf16[1024,768]{1,0:T(8,128)(2,1)S(1)} fusion(bf16[1024,768]{0,1:T(8,128)(2,1)S(1)} %pad_maximum_fusion.1, f32[768]{0:T(1024)S(1)} %get-tuple-element.149, bf16[512,1024]{1,0:T(8,128)(2,1)} %collective-permute-done.2, bf16[512,1024]{1,0:T(8,128)(2,1)} %fusion.23, pred[]{:T(512)S(6)} %eq.6), kind=kOutput, calls=%fused_computation.17 | convolution fusion | flops 1621622784 | bytes 5245953 | tf_op jit(solution)/shard_map/dot_general | solution.py:22
  75.4 9.1 %attn_fwd.3 = bf16[1024,256]{1,0:T(8,128)(2,1)S(1)} custom-call(s32[1024,1]{1,0:T(8,128)S(1)} %copy-done.6, s32[1,1024]{1,0:T(1,128)S(1)} %constant_dynamic-slice_fusion.segr_ref, bf16[1024,768]{1,0:T(8,128)(2,1)S(1)} %add_convert_fusion.1.q_ref.k_ref.v_ref, bf16[1024,768]{1,0:T(8,128)(2,1)S(1)} %add_convert_fusion.1.q_ref.k_ref.v_ref, ...), custom_call_target="tpu_custom_call" | custom-call | flops 1073741824 | bytes 3145728 | tf_op jit(solution)/shard_map/attn_fwd/pallas_call | solution.py:81
  85.0 1.4 add_convert_fusion.8
  86.9 1.5 collective-permute-start.10
  88.4 1.6 fusion.47
  90.0 2.0 fusion.68
  93.3 18.9 %collective-permute-done.10.g_a = bf16[512,1024]{1,0:T(8,128)(2,1)S(1)} collective-permute-done((bf16[512,1024]{1,0:T(8,128)(2,1)}, bf16[512,1024]{1,0:T(8,128)(2,1)S(1)}, u32[]{:S(2)}, u32[]{:S(2)}) %collective-permute-start.10) | collective-permute-done | bytes 1048608 | tf_op jit(solution)/shard_map/ppermute | solution.py:30
  112.3 1.5 collective-permute-start.9
  113.7 2.5 broadcast_4__act__pg.2._act
  116.3 2.5 broadcast_4__act__pg.2.clone._pg
  118.9 15.0 %ff_part.2 = (bf16[2048,1024]{1,0:T(8,128)(2,1)}, bf16[2048,1024]{1,0:T(8,128)(2,1)}, bf16[1024,1024]{1,0:T(8,128)(2,1)}, bf16[1024,1024]{1,0:T(8,128)(2,1)}, f32[1,1024]{1,0:T(1,128)S(1)}) custom-call(bf16[512,1024]{1,0:T(8,128)(2,1)S(1)} %add_convert_fusion.7.n_a, bf16[512,1024]{1,0:T(8,128)(2,1)} %copy-done.58, ...), custom_call_target="tpu_custom_call", output_to_operand_aliasing={{0}: (7, {}), {1}: (8, {})} | custom-call | flops 8589934592 | bytes 14680064 | tf_op jit(solution)/shard_map/ff_part/pallas_call | solution.py:242
  133.9 3.9 collective-permute-done.9.n_a
  137.8 2.7 collective-permute-done.12.n_b
  141.5 15.0 %ff_part.3 = (bf16[2048,1024]{1,0:T(8,128)(2,1)}, bf16[2048,1024]{1,0:T(8,128)(2,1)}, bf16[1024,1024]{1,0:T(8,128)(2,1)}, bf16[1024,1024]{1,0:T(8,128)(2,1)}, f32[1,1024]{1,0:T(1,128)S(1)}) custom-call(bf16[512,1024]{1,0:T(8,128)(2,1)S(1)} %collective-permute-done.9.n_a, bf16[512,1024]{1,0:T(8,128)(2,1)} %copy-done.60, ...), custom_call_target="tpu_custom_call", output_to_operand_aliasing={{0}: (7, {}), {1}: (8, {})} | custom-call | flops 8589934592 | bytes 14680064 | tf_op jit(solution)/shard_map/ff_part/pallas_call | solution.py:242
  156.5 2.4 slice.114
  159.1 8.0 %fusion.33 = bf16[1024,1024]{1,0:T(8,128)(2,1)} fusion(bf16[2048,1024]{1,0:T(8,128)(2,1)} %get-tuple-element.63, bf16[512,1024]{1,0:T(8,128)(2,1)S(1)} %copy-done.61, bf16[512,1024]{1,0:T(8,128)(2,1)S(1)} %collective-permute-done.9.n_a, bf16[512,1024]{1,0:T(8,128)(2,1)S(1)} %copy-done.59, bf16[512,1024]{1,0:T(8,128)(2,1)S(1)} %add_convert_fusion.7.n_a), kind=kOutput, calls=%fused_computation.57 | convolution fusion | flops 4312793088 | bytes 10485760 | tf_op jit(solution)/shard_map/dot_general | solution.py:22
  167.6 2.4 slice.112
  171.6 3.8 add_convert_fusion.6
  175.4 1.4 collective-permute-start.14
  176.8 7.8 %fusion.30 = bf16[1024,1024]{1,0:T(8,128)(2,1)} fusion(bf16[2048,1024]{1,0:T(8,128)(2,1)S(1)} %copy-done.34, bf16[512,1024]{1,0:T(8,128)(2,1)} %copy-done.57, bf16[512,1024]{1,0:T(8,128)(2,1)S(1)} %copy-done.56, bf16[512,1024]{1,0:T(8,128)(2,1)} %collective-permute-done.6.g_b, bf16[512,1024]{1,0:T(8,128)(2,1)} %g_a.1), kind=kOutput, calls=%fused_computation.56 | convolution fusion | flops 4312793088 | bytes 10485760 | tf_op jit(solution)/shard_map/dot_general | solution.py:22
  184.6 16.3 %collective-permute-done.14 = bf16[512,1024]{1,0:T(8,128)(2,1)} collective-permute-done((bf16[512,1024]{1,0:T(8,128)(2,1)}, bf16[512,1024]{1,0:T(8,128)(2,1)}, u32[]{:S(2)}, u32[]{:S(2)}) %collective-permute-start.14) | collective-permute-done | bytes 1048608 | tf_op jit(solution)/shard_map/ppermute | solution.py:30
  201.0 3.6 multiply_reduce_fusion
  204.7 4.3 %convert_reduce_fusion.2 = (f32[1024]{0:T(1024)S(1)}, bf16[512,1024]{1,0:T(8,128)(2,1)}, f32[512,1024]{1,0:T(8,128)}, f32[1024]{0:T(1024)S(1)}) fusion(f32[512]{0:T(512)S(1)} %get-tuple-element.154, f32[512,1024]{1,0:T(8,128)S(1)} %copy-done.21, f32[512]{0:T(512)S(1)} %broadcast_multiply_fusion.4, f32[512]{0:T(512)S(1)} %get-tuple-element.155, ...), kind=kLoop, calls=%fused_computation.44 | loop fusion | flops 9435136 | bytes 9457664 | tf_op jit(solution)/shard_map/reduce_sum | solution.py:576
  211.3 1.5 collective-permute-start.24
  212.8 1.9 add_convert_fusion.5
  215.5 3.3 maximum_select_fusion.1
  219.9 13.6 %attn_bwd.2 = (bf16[1024,768]{1,0:T(8,128)(2,1)S(1)}, f32[2,256]{1,0:T(2,128)S(1)}) custom-call(s32[1024,1]{1,0:T(8,128)S(1)} %copy-done.7, s32[1,1024]{1,0:T(1,128)S(1)} %constant_dynamic-slice_fusion.segr_ref, bf16[1024,768]{1,0:T(8,128)(2,1)S(1)} %add_convert_fusion.1.q_ref.k_ref.v_ref, bf16[1024,768]{1,0:T(8,128)(2,1)S(1)} %add_convert_fusion.1.q_ref.k_ref.v_ref, ...), custom_call_target="tpu_custom_call" | custom-call | flops 3221225472 | bytes 4718592 | tf_op jit(solution)/shard_map/attn_bwd/pallas_call | solution.py:159
  233.5 4.4 %convolution_convert_fusion = bf16[1024,768]{1,0:T(8,128)(2,1)S(1)} fusion(bf16[1024,768]{1,0:T(8,128)(2,1)S(1)} %get-tuple-element.65, bf16[512,1024]{1,0:T(8,128)(2,1)} %collective-permute-done.2, bf16[512,1024]{1,0:T(8,128)(2,1)} %fusion.23, pred[]{:T(512)S(6)} %eq.6), kind=kOutput, calls=%fused_computation.60 | convolution fusion | flops 1620836352 | bytes 5242881 | tf_op jit(solution)/shard_map/dot_general | solution.py:22
  237.9 1.4 collective-permute-start.16
  240.8 1.4 collective-permute-start.25
  242.1 2.3 fusion.41
  245.2 2.3 fusion.38
  247.5 13.6 %attn_bwd.3 = (bf16[1024,768]{1,0:T(8,128)(2,1)S(1)}, f32[2,256]{1,0:T(2,128)S(1)}) custom-call(s32[1024,1]{1,0:T(8,128)S(1)} %copy-done.7, s32[1,1024]{1,0:T(1,128)S(1)} %constant_dynamic-slice_fusion.segr_ref, bf16[1024,768]{1,0:T(8,128)(2,1)S(1)} %add_convert_fusion.2.q_ref.k_ref.v_ref, bf16[1024,768]{1,0:T(8,128)(2,1)S(1)} %add_convert_fusion.2.q_ref.k_ref.v_ref, ...), custom_call_target="tpu_custom_call" | custom-call | flops 3221225472 | bytes 4718592 | tf_op jit(solution)/shard_map/attn_bwd/pallas_call | solution.py:159
  261.2 24.1 %collective-permute-done.25 = f32[2,256]{1,0:T(2,128)S(1)} collective-permute-done((f32[2,256]{1,0:T(2,128)S(1)}, f32[2,256]{1,0:T(2,128)S(1)}, u32[]{:S(2)}, u32[]{:S(2)}) %collective-permute-start.25) | collective-permute-done | bytes 2080 | tf_op jit(solution)/shard_map/ppermute | solution.py:30
  285.3 2.0 add_convert_fusion.3
  288.0 1.2 concatenate.60
  289.2 4.9 %add_convert_fusion = bf16[1024,768]{1,0:T(8,128)(2,1)S(1)} fusion(bf16[1024,768]{1,0:T(8,128)(2,1)} %copy-done.54, bf16[1024,768]{1,0:T(8,128)(2,1)S(1)} %get-tuple-element.71, bf16[512,1024]{1,0:T(8,128)(2,1)} %collective-permute-done.2, bf16[512,1024]{1,0:T(8,128)(2,1)} %fusion.23, pred[]{:T(512)S(6)} %eq.6), kind=kOutput, calls=%fused_computation.16 | convolution fusion | flops 1622409216 | bytes 6815745 | tf_op jit(solution)/shard_map/dot_general | solution.py:22
  294.5 1.2 copy-done.22
  296.4 3.5 add_convert_fusion.4
  300.0 3.0 fusion.28
  304.5 1.5 collective-permute-start.22
  306.0 2.0 fusion.27
  310.2 84.1 %ring_sum.1 = (bf16[8,2,64,1024]{3,2,1,0:T(8,128)(2,1)S(1)}, f32[8,1,1024]{2,1,0:T(1,128)S(1)}, bf16[8,2,64,1024]{3,2,1,0:T(8,128)(2,1)S(1)}, bf16[8,2,64,1024]{3,2,1,0:T(8,128)(2,1)S(1)}) custom-call(bf16[8,2,64,1024]{3,2,1,0:T(8,128)(2,1)S(1)} %pad_maximum_fusion.x_ref, f32[8,1,1024]{2,1,0:T(1,128)S(1)} %reshape.161.small_ref, ...), custom_call_target="tpu_custom_call" | custom-call | tf_op jit(solution)/shard_map/ring_sum/pallas_call | solution.py:409
  394.6 1.1 copy-done.11
  396.9 1.6 copy.69
  398.5 3.2 copy.65
  401.8 2.6 bitcast_convert_fusion
  404.4 2.6 bitcast_convert_fusion.1
  407.0 1.3 reshape.173
  (230 shorter events, 25.7 us)
Async XLA Ops:
  7.2 18.1 %copy-start = (s32[2,1024]{1,0:T(2,128)S(1)}, s32[2,1024]{1,0:T(2,128)}, u32[]{:S(2)}) copy-start(s32[2,1024]{1,0:T(2,128)} %param.16) | copy-start | bytes 24580
  7.2 56.2 %all-gather.2.cloned.1.call-start = ((), (), s32[]{:S(2)}) async-start(), calls=%async_computation.2 | async-start | bytes 1179648 | tf_op jit(solution)/shard_map/all_gather | solution.py:506
  9.0 15.9 %copy-start.35 = (bf16[1024,3,256]{0,2,1:T(8,128)(2,1)}, bf16[1024,3,256]{0,2,1:T(8,128)(2,1)S(1)}, u32[]{:S(2)}) copy-start(bf16[1024,3,256]{0,2,1:T(8,128)(2,1)S(1)} %copy.53) | copy-start | bytes 4718596
  9.0 5.5 %copy-start.23 = (bf16[512,1024]{1,0:T(8,128)(2,1)S(1)}, bf16[512,1024]{1,0:T(8,128)(2,1)}, u32[]{:S(2)}) copy-start(bf16[512,1024]{1,0:T(8,128)(2,1)} %param.15) | copy-start | bytes 3145732
  9.8 11.9 %copy-start.48 = (f32[1024]{0:T(1024)S(1)}, f32[1024]{0:T(1024)}, u32[]{:S(2)}) copy-start(f32[1024]{0:T(1024)} %param.17) | copy-start | bytes 12292
  9.8 11.9 %copy-start.49 = (f32[1024]{0:T(1024)S(1)}, f32[1024]{0:T(1024)}, u32[]{:S(2)}) copy-start(f32[1024]{0:T(1024)} %param.18) | copy-start | bytes 12292
  11.5 9.3 %collective-permute-start = (bf16[64,1024]{0,1:T(8,128)(2,1)S(1)}, bf16[64,1024]{0,1:T(8,128)(2,1)S(1)}, u32[]{:S(2)}, u32[]{:S(2)}) collective-permute-start(bf16[64,1024]{0,1:T(8,128)(2,1)S(1)} %pad_maximum_fusion.4), channel_id=1, source_target_pairs={{0,2},{1,3},{2,0},{3,1},{4,6},{5,7},{6,4},{7,5},{8,10},{9,11},{10,... | collective-permute-start | bytes 393224 | tf_op jit(solution)/shard_map/ppermute | solution.py:30
  14.8 8.4 %copy-start.53 = (f32[2,256]{1,0:T(2,128)S(1)}, f32[2,256]{1,0:T(2,128)}, u32[]{:S(2)}) copy-start(f32[2,256]{1,0:T(2,128)} %param.20) | copy-start | bytes 6148
  21.7 286.6 %reduce-scatter.5.cloned.1.call-start = ((), (), s32[]{:S(2)}) async-start(), calls=%async_computation.4 | async-start | bytes 2359296 | tf_op jit(solution)/shard_map/reduce_scatter | solution.py:566
  23.1 3.8 collective-permute-start.2
  23.2 3.8 collective-permute-start.3
  26.4 25.5 %collective-permute-start.1 = (bf16[512,1024]{0,1:T(8,128)(2,1)}, bf16[512,1024]{0,1:T(8,128)(2,1)S(1)}, u32[]{:S(2)}, u32[]{:S(2)}) collective-permute-start(bf16[512,1024]{0,1:T(8,128)(2,1)} %pad_maximum_fusion.2), channel_id=1, source_target_pairs={{0,2},{1,3},{2,0},{3,1},{4,6},{5,7},{6,4},{7,5},{8,10},{9,11},{10,... | collective-permute-start | bytes 3145736 | tf_op jit(solution)/shard_map/ppermute | solution.py:30
  26.9 4.7 %copy-start.5 = (s32[1024,1]{1,0:T(8,128)}, s32[1024,1]{1,0:T(8,128)S(1)}, u32[]{:S(2)}) copy-start(s32[1024,1]{1,0:T(8,128)S(1)} %copy.59.segc_ref) | copy-start | bytes 12292
  51.9 15.0 %copy-start.38 = (bf16[512,1024]{0,1:T(8,128)(2,1)}, bf16[512,1024]{0,1:T(8,128)(2,1)S(1)}, u32[]{:S(2)}) copy-start(bf16[512,1024]{0,1:T(8,128)(2,1)S(1)} %collective-permute-done.1) | copy-start | bytes 3145732
  69.2 15.8 %copy-start.31 = (bf16[256,1024]{1,0:T(8,128)(2,1)}, bf16[256,1024]{1,0:T(8,128)(2,1)S(1)}, u32[]{:S(2)}) copy-start(bf16[256,1024]{1,0:T(8,128)(2,1)S(1)} %pad_maximum_fusion.3) | copy-start | bytes 1572868
  70.7 4.6 %copy-start.43 = (bf16[1024,768]{0,1:T(8,128)(2,1)}, bf16[1024,768]{0,1:T(8,128)(2,1)S(1)}, u32[]{:S(2)}) copy-start(bf16[1024,768]{0,1:T(8,128)(2,1)S(1)} %pad_maximum_fusion.1) | copy-start | bytes 4718596
  70.7 4.6 %copy-start.6 = (s32[1024,1]{1,0:T(8,128)S(1)}, s32[1024,1]{1,0:T(8,128)}, u32[]{:S(2)}) copy-start(s32[1024,1]{1,0:T(8,128)} %copy-done.5) | copy-start | bytes 12292
  75.3 9.1 %copy-start.3 = (bf16[1024,256]{1,0:T(8,128)(2,1)S(1)}, bf16[1024,256]{1,0:T(8,128)(2,1)}, u32[]{:S(2)}) copy-start(bf16[1024,256]{1,0:T(8,128)(2,1)} %copy-done.2) | copy-start | bytes 1572868
  75.3 9.1 %copy-start.29 = (bf16[256,1024]{1,0:T(8,128)(2,1)S(1)}, bf16[256,1024]{1,0:T(8,128)(2,1)}, u32[]{:S(2)}) copy-start(bf16[256,1024]{1,0:T(8,128)(2,1)} %param.21) | copy-start | bytes 1572868
  86.4 3.6 collective-permute-start.4
  86.4 27.4 %collective-permute-start.6 = (bf16[512,1024]{1,0:T(8,128)(2,1)}, bf16[512,1024]{1,0:T(8,128)(2,1)}, u32[]{:S(2)}, u32[]{:S(2)}) collective-permute-start(bf16[512,1024]{1,0:T(8,128)(2,1)} %g_a.1), channel_id=1, source_target_pairs={{0,1},{1,0},{2,3},{3,2},{4,5},{5,4},{6,7},{7,6},{8,9},{9,8},{10,11... | collective-permute-start | bytes 3145736 | tf_op jit(solution)/shard_map/ppermute | solution.py:30
  86.9 25.4 %collective-permute-start.10 = (bf16[512,1024]{1,0:T(8,128)(2,1)}, bf16[512,1024]{1,0:T(8,128)(2,1)S(1)}, u32[]{:S(2)}, u32[]{:S(2)}) collective-permute-start(bf16[512,1024]{1,0:T(8,128)(2,1)} %g_a.1), channel_id=1, source_target_pairs={{0,2},{1,3},{2,0},{3,1},{4,6},{5,7},{6,4},{7,5},{8,10},{9,11},{10,... | collective-permute-start | bytes 3145736 | tf_op jit(solution)/shard_map/ppermute | solution.py:30
  93.3 20.4 %collective-permute-start.5 = (bf16[512,1024]{1,0:T(8,128)(2,1)S(1)}, bf16[512,1024]{1,0:T(8,128)(2,1)S(1)}, u32[]{:S(2)}, u32[]{:S(2)}) collective-permute-start(bf16[512,1024]{1,0:T(8,128)(2,1)S(1)} %add_convert_fusion.7.n_a), channel_id=1, source_target_pairs={{0,1},{1,0},{2,3},{3,2},{4,5},{5,4},{6,7},{7,6},{8,9},{9,8},{10,11... | collective-permute-start | bytes 3145736 | tf_op jit(solution)/shard_map/ppermute | solution.py:30
  112.3 4.0 copy-start.55
  112.3 21.6 %collective-permute-start.11 = (bf16[512,1024]{1,0:T(8,128)(2,1)S(1)}, bf16[512,1024]{1,0:T(8,128)(2,1)S(1)}, u32[]{:S(2)}, u32[]{:S(2)}) collective-permute-start(bf16[512,1024]{1,0:T(8,128)(2,1)S(1)} %collective-permute-done.10.g_a), channel_id=1, source_target_pairs={{0,1},{1,0},{2,3},{3,2},{4,5},{5,4},{6,7},{7,6},{8,9},{9,8},{10,11... | collective-permute-start | bytes 3145736 | tf_op jit(solution)/shard_map/ppermute | solution.py:30
  112.3 25.6 %collective-permute-start.9 = (bf16[512,1024]{1,0:T(8,128)(2,1)S(1)}, bf16[512,1024]{1,0:T(8,128)(2,1)S(1)}, u32[]{:S(2)}, u32[]{:S(2)}) collective-permute-start(bf16[512,1024]{1,0:T(8,128)(2,1)S(1)} %add_convert_fusion.7.n_a), channel_id=1, source_target_pairs={{0,2},{1,3},{2,0},{3,1},{4,6},{5,7},{6,4},{7,5},{8,10},{9,11},{10,... | collective-permute-start | bytes 3145736 | tf_op jit(solution)/shard_map/ppermute | solution.py:30
  133.9 6.6 %copy-start.57 = (bf16[512,1024]{1,0:T(8,128)(2,1)}, bf16[512,1024]{1,0:T(8,128)(2,1)S(1)}, u32[]{:S(2)}) copy-start(bf16[512,1024]{1,0:T(8,128)(2,1)S(1)} %collective-permute-done.11.g_b) | copy-start | bytes 3145732
  137.8 2.7 collective-permute-start.12
  158.9 12.7 %collective-permute-start.13 = (bf16[512,1024]{1,0:T(8,128)(2,1)}, bf16[512,1024]{1,0:T(8,128)(2,1)}, u32[]{:S(2)}, u32[]{:S(2)}) collective-permute-start(bf16[512,1024]{1,0:T(8,128)(2,1)} %slice.114), channel_id=1, source_target_pairs={{0,1},{1,0},{2,3},{3,2},{4,5},{5,4},{6,7},{7,6},{8,9},{9,8},{10,11... | collective-permute-start | bytes 3145736 | tf_op jit(solution)/shard_map/ppermute | solution.py:30
  167.1 141.2 %reduce-scatter.3.cloned.1.call-start = ((), (), s32[]{:S(2)}) async-start(), calls=%async_computation.3 | async-start | bytes 2359296 | tf_op jit(solution)/shard_map/reduce_scatter | solution.py:564
  170.0 30.9 %collective-permute-start.8 = (bf16[512,1024]{1,0:T(8,128)(2,1)}, bf16[512,1024]{1,0:T(8,128)(2,1)}, u32[]{:S(2)}, u32[]{:S(2)}) collective-permute-start(bf16[512,1024]{1,0:T(8,128)(2,1)} %slice.112), channel_id=1, source_target_pairs={{0,1},{1,0},{2,3},{3,2},{4,5},{5,4},{6,7},{7,6},{8,9},{9,8},{10,11... | collective-permute-start | bytes 3145736 | tf_op jit(solution)/shard_map/ppermute | solution.py:30
  170.4 6.4 %copy-start.34 = (bf16[2048,1024]{1,0:T(8,128)(2,1)S(1)}, bf16[2048,1024]{1,0:T(8,128)(2,1)}, u32[]{:S(2)}) copy-start(bf16[2048,1024]{1,0:T(8,128)(2,1)} %get-tuple-element.62) | copy-start | bytes 12582916
  171.4 5.4 %copy-start.56 = (bf16[512,1024]{1,0:T(8,128)(2,1)S(1)}, bf16[512,1024]{1,0:T(8,128)(2,1)}, u32[]{:S(2)}) copy-start(bf16[512,1024]{1,0:T(8,128)(2,1)} %copy-done.55) | copy-start | bytes 3145732
  171.4 41.4 %collective-permute-start.18 = (bf16[512,1024]{1,0:T(8,128)(2,1)}, bf16[512,1024]{1,0:T(8,128)(2,1)}, u32[]{:S(2)}, u32[]{:S(2)}) collective-permute-start(bf16[512,1024]{1,0:T(8,128)(2,1)} %slice.116), channel_id=1, source_target_pairs={{0,1},{1,0},{2,3},{3,2},{4,5},{5,4},{6,7},{7,6},{8,9},{9,8},{10,11... | collective-permute-start | bytes 3145736 | tf_op jit(solution)/shard_map/ppermute | solution.py:30
  175.4 25.6 %collective-permute-start.14 = (bf16[512,1024]{1,0:T(8,128)(2,1)}, bf16[512,1024]{1,0:T(8,128)(2,1)}, u32[]{:S(2)}, u32[]{:S(2)}) collective-permute-start(bf16[512,1024]{1,0:T(8,128)(2,1)} %add_convert_fusion.6), channel_id=1, source_target_pairs={{0,2},{1,3},{2,0},{3,1},{4,6},{5,7},{6,4},{7,5},{8,10},{9,11},{10,... | collective-permute-start | bytes 3145736 | tf_op jit(solution)/shard_map/ppermute | solution.py:30
  184.6 20.0 %copy-start.21 = (f32[512,1024]{1,0:T(8,128)S(1)}, f32[512,1024]{1,0:T(8,128)}, u32[]{:S(2)}) copy-start(f32[512,1024]{1,0:T(8,128)} %copy-done.20) | copy-start | bytes 6291460
  184.6 20.0 %copy-start.27 = (bf16[1024,1024]{1,0:T(8,128)(2,1)S(1)}, bf16[1024,1024]{1,0:T(8,128)(2,1)}, u32[]{:S(2)}) copy-start(bf16[1024,1024]{1,0:T(8,128)(2,1)} %get-tuple-element.53) | copy-start | bytes 6291460
  204.6 4.9 %copy-start.40 = (bf16[1024,1024]{1,0:T(8,128)(2,1)S(1)}, bf16[1024,1024]{1,0:T(8,128)(2,1)}, u32[]{:S(2)}) copy-start(bf16[1024,1024]{1,0:T(8,128)(2,1)} %get-tuple-element.52) | copy-start | bytes 6291460
  208.9 6.5 %collective-permute-start.15 = (bf16[512,1024]{1,0:T(8,128)(2,1)}, bf16[512,1024]{1,0:T(8,128)(2,1)}, u32[]{:S(2)}, u32[]{:S(2)}) collective-permute-start(bf16[512,1024]{1,0:T(8,128)(2,1)} %get-tuple-element.133), channel_id=1, source_target_pairs={{0,1},{1,0},{2,3},{3,2},{4,5},{5,4},{6,7},{7,6},{8,9},{9,8},{10,11... | collective-permute-start | bytes 3145736 | tf_op jit(solution)/shard_map/ppermute | solution.py:30
  209.0 2.3 collective-permute-start.23
  210.6 83.9 %collective-permute-start.7 = (bf16[512,1024]{1,0:T(8,128)(2,1)}, bf16[512,1024]{1,0:T(8,128)(2,1)}, u32[]{:S(2)}, u32[]{:S(2)}) collective-permute-start(bf16[512,1024]{1,0:T(8,128)(2,1)} %slice.110), channel_id=1, source_target_pairs={{0,1},{1,0},{2,3},{3,2},{4,5},{5,4},{6,7},{7,6},{8,9},{9,8},{10,11... | collective-permute-start | bytes 3145736 | tf_op jit(solution)/shard_map/ppermute | solution.py:30
  211.3 4.1 collective-permute-start.24
  214.7 70.5 %collective-permute-start.19 = (bf16[512,1024]{1,0:T(8,128)(2,1)S(1)}, bf16[512,1024]{1,0:T(8,128)(2,1)S(1)}, u32[]{:S(2)}, u32[]{:S(2)}) collective-permute-start(bf16[512,1024]{1,0:T(8,128)(2,1)S(1)} %add_convert_fusion.5), channel_id=1, source_target_pairs={{0,2},{1,3},{2,0},{3,1},{4,6},{5,7},{6,4},{7,5},{8,10},{9,11},{10,... | collective-permute-start | bytes 3145736 | tf_op jit(solution)/shard_map/ppermute | solution.py:30
  233.5 5.9 %copy-start.10 = (bf16[1024,256]{1,0:T(8,128)(2,1)S(1)}, bf16[1024,256]{1,0:T(8,128)(2,1)}, u32[]{:S(2)}) copy-start(bf16[1024,256]{1,0:T(8,128)(2,1)} %copy-done.8) | copy-start | bytes 1572868
  237.9 4.3 %copy-start.44 = (bf16[1024,768]{0,1:T(8,128)(2,1)S(1)}, bf16[1024,768]{0,1:T(8,128)(2,1)}, u32[]{:S(2)}) copy-start(bf16[1024,768]{0,1:T(8,128)(2,1)} %copy-done.43) | copy-start | bytes 4718596
  237.9 47.4 %collective-permute-start.16 = (bf16[1024,768]{1,0:T(8,128)(2,1)S(1)}, bf16[1024,768]{1,0:T(8,128)(2,1)S(1)}, u32[]{:S(2)}, u32[]{:S(2)}) collective-permute-start(bf16[1024,768]{1,0:T(8,128)(2,1)S(1)} %convolution_convert_fusion), channel_id=1, source_target_pairs={{0,2},{1,3},{2,0},{3,1},{4,6},{5,7},{6,4},{7,5},{8,10},{9,11},{10,... | collective-permute-start | bytes 4718600 | tf_op jit(solution)/shard_map/ppermute | solution.py:30
  240.0 45.2 %collective-permute-start.17 = (bf16[256,1024]{1,0:T(8,128)(2,1)S(1)}, bf16[256,1024]{1,0:T(8,128)(2,1)S(1)}, u32[]{:S(2)}, u32[]{:S(2)}) collective-permute-start(bf16[256,1024]{1,0:T(8,128)(2,1)S(1)} %convolution_convert_fusion.2), channel_id=1, source_target_pairs={{0,2},{1,3},{2,0},{3,1},{4,6},{5,7},{6,4},{7,5},{8,10},{9,11},{10,... | collective-permute-start | bytes 1572872 | tf_op jit(solution)/shard_map/ppermute | solution.py:30
  240.8 3.7 copy-start.30
  240.8 44.5 %collective-permute-start.25 = (f32[2,256]{1,0:T(2,128)S(1)}, f32[2,256]{1,0:T(2,128)S(1)}, u32[]{:S(2)}, u32[]{:S(2)}) collective-permute-start(f32[2,256]{1,0:T(2,128)S(1)} %get-tuple-element.77), channel_id=1, source_target_pairs={{0,2},{1,3},{2,0},{3,1},{4,6},{5,7},{6,4},{7,5},{8,10},{9,11},{10,... | collective-permute-start | bytes 6152 | tf_op jit(solution)/shard_map/ppermute | solution.py:30
  247.5 37.7 %copy-start.36 = (bf16[1024,3,256]{0,2,1:T(8,128)(2,1)S(1)}, bf16[1024,3,256]{0,2,1:T(8,128)(2,1)}, u32[]{:S(2)}) copy-start(bf16[1024,3,256]{0,2,1:T(8,128)(2,1)} %copy-done.35) | copy-start | bytes 4718596
  247.5 37.8 %copy-start.62 = (f32[512,1024]{1,0:T(8,128)S(1)}, f32[512,1024]{1,0:T(8,128)}, u32[]{:S(2)}) copy-start(f32[512,1024]{1,0:T(8,128)} %fusion.38) | copy-start | bytes 6291460
  261.2 28.0 %copy-start.18 = (bf16[1024,768]{1,0:T(8,128)(2,1)}, bf16[1024,768]{1,0:T(8,128)(2,1)S(1)}, u32[]{:S(2)}) copy-start(bf16[1024,768]{1,0:T(8,128)(2,1)S(1)} %get-tuple-element.71) | copy-start | bytes 4718596
  287.3 12.7 %collective-permute-start.20 = (bf16[512,1024]{1,0:T(8,128)(2,1)}, bf16[512,1024]{1,0:T(8,128)(2,1)}, u32[]{:S(2)}, u32[]{:S(2)}) collective-permute-start(bf16[512,1024]{1,0:T(8,128)(2,1)} %add_convert_fusion.3), channel_id=1, source_target_pairs={{0,1},{1,0},{2,3},{3,2},{4,5},{5,4},{6,7},{7,6},{8,9},{9,8},{10,11... | collective-permute-start | bytes 3145736 | tf_op jit(solution)/shard_map/ppermute | solution.py:30
  289.2 4.9 %copy-start.42 = (bf16[8,2,64,256]{3,2,1,0:T(8,128)(2,1)S(1)}, bf16[8,2,64,256]{3,2,1,0:T(8,128)(2,1)}, u32[]{:S(2)}) copy-start(bf16[8,2,64,256]{3,2,1,0:T(8,128)(2,1)} %concatenate.60) | copy-start | bytes 1572868
  289.2 5.3 %copy-start.46 = (bf16[512,1024]{1,0:T(8,128)(2,1)S(1)}, bf16[512,1024]{1,0:T(8,128)(2,1)}, u32[]{:S(2)}) copy-start(bf16[512,1024]{1,0:T(8,128)(2,1)} %copy-done.45) | copy-start | bytes 3145732
  289.2 5.3 %copy-start.52 = (f32[1024]{0:T(1024)S(1)}, f32[1024]{0:T(1024)}, u32[]{:S(2)}) copy-start(f32[1024]{0:T(1024)} %param.28) | copy-start | bytes 12292
  294.4 5.5 %copy-start.19 = (bf16[1024,768]{1,0:T(8,128)(2,1)S(1)}, bf16[1024,768]{1,0:T(8,128)(2,1)}, u32[]{:S(2)}) copy-start(bf16[1024,768]{1,0:T(8,128)(2,1)} %copy-done.18) | copy-start | bytes 4718596
  294.4 5.5 %copy-start.25 = (bf16[512,1024]{1,0:T(8,128)(2,1)S(1)}, bf16[512,1024]{1,0:T(8,128)(2,1)}, u32[]{:S(2)}) copy-start(bf16[512,1024]{1,0:T(8,128)(2,1)} %param.15) | copy-start | bytes 3145732
  294.4 5.5 %copy-start.37 = (bf16[1024,3,256]{0,2,1:T(8,128)(2,1)S(1)}, bf16[1024,3,256]{0,2,1:T(8,128)(2,1)}, u32[]{:S(2)}) copy-start(bf16[1024,3,256]{0,2,1:T(8,128)(2,1)} %copy-done.35) | copy-start | bytes 4718596
  294.5 5.5 %copy-start.63 = (f32[512,1024]{1,0:T(8,128)S(1)}, f32[512,1024]{1,0:T(8,128)}, u32[]{:S(2)}) copy-start(f32[512,1024]{1,0:T(8,128)} %fusion.41) | copy-start | bytes 6291460
  299.9 6.1 %copy-start.26 = (f32[512,1024]{1,0:T(8,128)S(1)}, f32[512,1024]{1,0:T(8,128)}, u32[]{:S(2)}) copy-start(f32[512,1024]{1,0:T(8,128)} %get-tuple-element.134) | copy-start | bytes 6291460
  303.0 1.4 collective-permute-start.21
  304.5 3.7 collective-permute-start.22
  404.4 4.5 %copy-start.1 = (s32[2,1024]{1,0:T(2,128)S(1)}, s32[2,1024]{1,0:T(2,128)}, u32[]{:S(2)}) copy-start(s32[2,1024]{1,0:T(2,128)} %param.16) | copy-start | bytes 24580
  (31 other events, 65.4 us)
Sparse Core Ops, SparseCore 0:
  21.8 41.5 all-gather.1
  167.2 66.5 reduce-scatter.4
  237.4 66.7 reduce-scatter.2

commit v2 on v1

--- a/solution.py
+++ b/solution.py
@@ -14,6 +14,7 @@
 BF = jnp.bfloat16
 F32 = jnp.float32
 SCALE = HD ** (-0.5)
+MESH_ID = pl.DeviceIdType.MESH
 NT = (((1,), (1,)), ((), ()))
 TN = (((0,), (0,)), ((), ()))
 
@@ -195,84 +196,212 @@
 
 
 def ff_kernel(
-    half, n_a, n_b, g_a, g_b, we_ref, wr_ref, be_ref, _act, _pg, act_ref, pg_ref, branch_ref, ng_ref, sum_ref
+    n2_ref, og_ref, we_ref, wr_ref, be_ref, resid_ref, gain_ref,
+    rgrad_ref, mg_ref, rg_ref, eg_ref, brn_ref, brf_ref, usum_ref, dsum_ref,
+    n2b, act, pg, ng, br, ng_d, br_d, ng_s, br_s, ng_far, ng_out,
+    send, recv,
 ):
-    i = pl.program_id(0)
-    first = i < half
-    rows = jnp.where(first, n_a[...], n_b[...])
-    grads = jnp.where(first, g_a[...], g_b[...])
-    u = dot(rows, we_ref[...]) + be_ref[...]
-    act_grad = dot(grads, wr_ref[...], NT)
-    sq = u * u
-    th = jnp.tanh(u * (GA + (GA * GB) * sq))
-    cdf = 0.5 * (1.0 + th)
-    act = (u * cdf).astype(BF)
-    slope = cdf + (0.5 * u) * (1.0 - th * th) * (GA + (3.0 * GA * GB) * sq)
-    pre = (act_grad * slope).astype(BF)
-    act_ref[...] = act
-    pg_ref[...] = pre
-    branch_ref[...] = dot(act, wr_ref[...]).astype(BF)
-    ng_ref[...] = dot(pre, we_ref[...], NT).astype(BF)
-
-    @pl.when(i == 0)
-    def _():
-        sum_ref[...] = jnp.zeros_like(sum_ref)
-
-    sum_ref[...] += jnp.sum(pre.astype(F32), axis=0, keepdims=True)
-
-
-def ff_part(part, n_a, n_b, g_a, g_b, we, wr, be, act, pg):
-    rows, width = n_a.shape
+    rows, width = n2_ref.shape
+    units = we_ref.shape[1]
+    part = rows // 2
+    nb = 256
+    me = lax.axis_index("tensor")
+    core = me % 2
+    sib = me + 1 - 2 * core
+    far = (me + 2) % 4
+
+    barrier = pltpu.get_barrier_semaphore()
+    for other in (sib, far):
+        pl.semaphore_signal(barrier, inc=1, device_id={"tensor": other}, device_id_type=MESH_ID)
+    pl.semaphore_wait(barrier, 2)
+
+    def remote(src, dst, k, other):
+        return pltpu.make_async_remote_copy(
+            src_ref=src,
+            dst_ref=dst,
+            send_sem=send.at[k],
+            recv_sem=recv.at[k],
+            device_id={"tensor": other},
+            device_id_type=MESH_ID,
+        )
+
+    def y_at(c):
+        return pl.ds((2 + c) * rows, part)
+
+    def d_at(c):
+        return pl.ds((2 + c) * rows + part, part)
+
+    def rows_across(c):
+        return remote(n2_ref.at[pl.ds(c * part, part)], n2b.at[y_at(c)], c, far)
+
+    def rows_beside():
+        return remote(n2_ref, n2b.at[pl.ds(rows, rows)], 2, sib)
+
+    def rows_forward(c):
+        return remote(n2b.at[y_at(c)], n2b.at[d_at(c)], 3 + c, sib)
+
+    def ng_beside():
+        return remote(ng.at[pl.ds(rows, rows)], ng_s, 5, sib)
+
+    def br_beside():
+        return remote(br.at[pl.ds(rows, rows)], br_s, 6, sib)
+
+    def ng_combine(c):
+        return remote(ng.at[d_at(c)], ng_d.at[c], 7 + c, sib)
+
+    def br_combine(c):
+        return remote(br.at[d_at(c)], br_d.at[c], 9 + c, sib)
+
+    def ng_across(c):
+        return remote(ng_out.at[c], ng_far.at[c], 11 + c, far)
+
+    def mg_beside(c):
+        at = pl.ds(pl.multiple_of(core * rows + c * part, part), part)
+        return remote(mg_ref.at[at], mg_ref.at[at], 13 + c, sib)
+
+    for c in range(2):
+        rows_across(c).start()
+    rows_beside().start()
+    n2b[0:rows, :] = n2_ref[...]
+    usum_ref[...] = jnp.zeros_like(usum_ref)
+
+    @pl.loop(0, 4)
+    def _(b):
+        at = pl.ds(pl.multiple_of(b * rows, rows), rows)
+        c = b - 2
+
+        @pl.when(b == 1)
+        def _():
+            rows_beside().wait()
+
+        @pl.when(b >= 2)
+        def _():
+            rows_across(c).wait()
+            rows_forward(c).start()
+            rows_forward(c).wait()
+
+        for k in range(units // nb):
+            cols = slice(k * nb, (k + 1) * nb)
+            u = dot(n2b[at, :], we_ref[:, cols]) + be_ref[:, cols]
+            act_grad = dot(og_ref[at, :], wr_ref[cols, :], NT)
+            sq = u * u
+            th = jnp.tanh(u * (GA + (GA * GB) * sq))
+            cdf = 0.5 * (1.0 + th)
+            slope = cdf + (0.5 * u) * (1.0 - th * th) * (GA + (3.0 * GA * GB) * sq)
+            pre = (act_grad * slope).astype(BF)
+            act[at, cols] = (u * cdf).astype(BF)
+            pg[at, cols] = pre
+            usum_ref[:, cols] += jnp.sum(pre.astype(F32), axis=0, keepdims=True)
+        for k in range(width // nb):
+            cols = slice(k * nb, (k + 1) * nb)
+            ng[at, cols] = dot(pg[at, :], we_ref[cols, :], NT).astype(BF)
+
+        @pl.when(b == 1)
+        def _():
+            ng_beside().start()
+
+        @pl.when(b >= 2)
+        def _():
+            ng_combine(c).start()
+
+        for k in range(width // nb):
+            cols = slice(k * nb, (k + 1) * nb)
+            br[at, cols] = dot(act[at, :], wr_ref[:, cols]).astype(BF)
+
+        @pl.when(b == 1)
+        def _():
+            br_beside().start()
+
+        @pl.when(b >= 2)
+        def _():
+            br_combine(c).start()
+            ng_combine(c).wait()
+            ng_out[c] = (ng[y_at(c), :].astype(F32) + ng_d[c].astype(F32)).astype(BF)
+            ng_across(c).start()
+
+    @pl.loop(0, width // nb)
+    def _(k):
+        cols = pl.ds(pl.multiple_of(k * nb, nb), nb)
+        rg_ref[:, cols] = dot(act[...], og_ref[:, cols], TN).astype(BF)
+        eg_ref[:, cols] = dot(n2b[...], pg[:, cols], TN).astype(BF)
+
+    br_beside().wait()
+    brn_ref[...] = (br[0:rows, :].astype(F32) + br_s[...].astype(F32)).astype(BF)
+    for c in range(2):
+        br_combine(c).wait()
+        brf_ref[c * part : (c + 1) * part, :] = (
+            br[y_at(c), :].astype(F32) + br_d[c].astype(F32)
+        ).astype(BF)
+    ng_beside().wait()
+    dsum_ref[...] = jnp.zeros_like(dsum_ref)
+    step = 64
+    for c in range(2):
+        ng_across(c).wait()
+
+        @pl.loop(0, part // step)
+        def _(r):
+            inner = pl.ds(pl.multiple_of(r * step, step), step)
+            at = pl.ds(pl.multiple_of(c * part + r * step, step), step)
+            grad = ng[at, :].astype(F32) + ng_s[at, :].astype(F32) + ng_far[c, inner, :].astype(F32)
+            normed, scale = norm_stats(resid_ref[at, :])
+            g = grad * gain_ref[...]
+            gn = g * normed
+            mean_g = jnp.mean(g, axis=-1, keepdims=True)
+            mean_gn = jnp.mean(gn, axis=-1, keepdims=True)
+            og = og_ref[at, :].astype(F32)
+            rgrad = og + scale * (g - mean_g - normed * mean_gn)
+            rgrad_ref[at, :] = rgrad
+            mg = rgrad.astype(BF)
+            mg_ref[pl.ds(pl.multiple_of(core * rows + c * part + r * step, step), step), :] = mg
+            dsum_ref[0:1, :] += jnp.sum(mg.astype(F32), axis=0, keepdims=True)
+            dsum_ref[1:2, :] += jnp.sum(grad * normed, axis=0, keepdims=True)
+            dsum_ref[2:3, :] += jnp.sum(grad, axis=0, keepdims=True)
+            dsum_ref[3:4, :] += jnp.sum(og, axis=0, keepdims=True)
+
+        mg_beside(c).start()
+    for c in range(2):
+        mg_beside(c).wait()
+
+
+def ff(n2, og_all, we, wr, be, resid, gain):
+    rows, width = n2.shape
     units = we.shape[1]
-    block = 256
-    half = rows // block
-    base = 2 * half * part
-
-    def lo():
-        return pl.BlockSpec((block, width), lambda i: (jnp.minimum(i, half - 1), 0))
-
-    def hi():
-        return pl.BlockSpec((block, width), lambda i: (jnp.maximum(i - half, 0), 0))
-
-    def whole(a):
-        return pl.BlockSpec(a.shape, lambda i: (0, 0), pipeline_mode=pl.Buffered(1))
-
-    here = pl.BlockSpec((block, units), lambda i: (i + base, 0))
-    out = pl.BlockSpec((block, width), lambda i: (i, 0))
+    part = rows // 2
+    vmem = pl.BlockSpec(memory_space=pltpu.VMEM)
     return pl.pallas_call(
-        functools.partial(ff_kernel, half),
-        grid=(2 * half,),
-        in_specs=[
-            lo(),
-            hi(),
-            lo(),
-            hi(),
-            whole(we),
-            whole(wr),
-            whole(be),
-            pl.BlockSpec(memory_space=pl.ANY),
-            pl.BlockSpec(memory_space=pl.ANY),
-        ],
-        out_specs=[here, here, out, out, pl.BlockSpec((1, units), lambda i: (0, 0))],
+        ff_kernel,
+        in_specs=[vmem] * 7,
+        out_specs=[vmem] * 8,
         out_shape=[
-            jax.ShapeDtypeStruct(act.shape, BF),
-            jax.ShapeDtypeStruct(pg.shape, BF),
+            jax.ShapeDtypeStruct((rows, width), F32),
             jax.ShapeDtypeStruct((2 * rows, width), BF),
-            jax.ShapeDtypeStruct((2 * rows, width), BF),
+            jax.ShapeDtypeStruct((units, width), BF),
+            jax.ShapeDtypeStruct((width, units), BF),
+            jax.ShapeDtypeStruct((rows, width), BF),
+            jax.ShapeDtypeStruct((rows, width), BF),
             jax.ShapeDtypeStruct((1, units), F32),
-        ],
-        input_output_aliases={7: 0, 8: 1},
-        compiler_params=pltpu.CompilerParams(vmem_limit_bytes=52 << 20),
-        cost_estimate=pl.CostEstimate(
-            flops=16 * rows * width * units,
-            bytes_accessed=4 * width * units + 20 * rows * width,
-            transcendentals=2 * rows * units,
+            jax.ShapeDtypeStruct((4, width), F32),
+        ],
+        scratch_shapes=[
+            pltpu.VMEM((4 * rows, width), BF),
+            pltpu.VMEM((4 * rows, units), BF),
+            pltpu.VMEM((4 * rows, units), BF),
+            pltpu.VMEM((4 * rows, width), BF),
+            pltpu.VMEM((4 * rows, width), BF),
+            pltpu.VMEM((2, part, width), BF),
+            pltpu.VMEM((2, part, width), BF),
+            pltpu.VMEM((rows, width), BF),
+            pltpu.VMEM((rows, width), BF),
+            pltpu.VMEM((2, part, width), BF),
+            pltpu.VMEM((2, part, width), BF),
+            pltpu.SemaphoreType.DMA((15,)),
+            pltpu.SemaphoreType.DMA((15,)),
+        ],
+        compiler_params=pltpu.CompilerParams(
+            collective_id=2, has_side_effects=True, vmem_limit_bytes=60 << 20
         ),
-        name="ff_part",
-    )(n_a, n_b, g_a, g_b, we, wr, be, act, pg)
-
-
-MESH_ID = pl.DeviceIdType.MESH
+        name="ff",
+    )(n2, og_all, we, wr, be, resid, gain)
 
 
 def ring_kernel(
@@ -488,6 +617,14 @@
     dp_size = lax.axis_size("dp")
     dp_place = lax.axis_index("dp")
 
+    half = rows // 2
+    og_y = swap(out_grad, 2)
+    og_s = swap(out_grad, 1)
+    og_d = swap(og_y, 1)
+    og_all = jnp.concatenate(
+        [out_grad, og_s, og_y[:half], og_d[:half], og_y[half:], og_d[half:]], axis=0
+    )
+
     wq = w_qkv.reshape(width, 3 * cols)
     top = width // 2
     mid = cols // 2
@@ -504,7 +641,7 @@
     )
     piece = swap(far_half, 2)
     low = lax.all_gather(piece, "dp", axis=0, tiled=True)
-    near_half = after(near_half, piece)
+    near_half = after(near_half, og_y)
     high = swap(near_half, 2)
     qb_far = swap(qv_bias, 2)
     wq_far = jnp.concatenate([high[:, : 3 * cols], low[:, : 3 * cols]], axis=0)
@@ -531,51 +668,17 @@
     got = swap(part.astype(BF), 1)
     mixed = dot(own_rows(att_a), w_mix) + dot(own_rows(att_b), wm_far) + got.astype(F32) + mix_bias
     resid = x + mixed
-    norm2, scale2 = norm_stats(resid)
+    norm2 = norm_stats(resid)[0]
     n2 = (norm2 * second_gain + second_shift).astype(BF)
 
-    og_s = swap(out_grad, 1)
-    og_y = swap(after(out_grad, high), 2)
-    og_d = swap(og_y, 1)
-
-    n2_y = swap(n2, 2)
-    n2_s = swap(n2, 1)
-
-    be = expand_bias.reshape(1, units)
-    act = jnp.zeros((4 * rows, units), BF)
-    pg = jnp.zeros((4 * rows, units), BF)
-    act, pg, br0, ng0, sum0 = ff_part(0, n2, n2_s, out_grad, og_s, w_expand, w_reduce, be, act, pg)
-    n2_y, og_y, og_d, act = lax.optimization_barrier((n2_y, og_y, og_d, act))
-    n2_d = swap(n2_y, 1)
-    act, pg, br1, ng1, sum1 = ff_part(1, n2_y, n2_d, og_y, og_d, w_expand, w_reduce, be, act, pg)
-
-    def across(far):
-        return (far[:rows].astype(F32) + swap(far[rows:], 1).astype(F32)).astype(BF)
-
-    def near_sum(near):
-        return near[:rows].astype(F32) + swap(near[rows:], 1).astype(F32)
-
-    ng_got = swap(across(ng1), 2)
-    br_got = swap(after(across(br1), ng_got), 2)
-
-    grads_all = jnp.concatenate([out_grad, og_s, og_y, og_d], axis=0)
-    n2_all = jnp.concatenate([n2, n2_s, n2_y, n2_d], axis=0)
-    reduce_grad = dot(act, grads_all, TN).astype(BF)
+    flat = (1, width)
+    resid_grad, mg_all, reduce_grad, expand_grad, br_near, br_far, unit_sums, sums2 = ff(
+        n2, og_all, w_expand, w_reduce, expand_bias.reshape(1, units), resid, second_gain.reshape(flat)
+    )
+    br_got = swap(br_far, 2)
     reduce_own = lax.psum_scatter(reduce_grad, "dp", scatter_dimension=0, tiled=True)
-    expand_grad = dot(n2_all, pg, TN).astype(BF)
     expand_own = lax.psum_scatter(expand_grad, "dp", scatter_dimension=0, tiled=True)
-    expand_bias_grad = (sum0 + sum1)[0]
-
-    ng_got, reduce_grad, expand_grad = lax.optimization_barrier((ng_got, reduce_grad, expand_grad))
-    ng = near_sum(ng0) + ng_got.astype(F32)
-    grad = out_grad.astype(F32)
-    reduce_bias_grad = jnp.sum(grad, axis=0)
-    back2, second_gain_grad, second_shift_grad = norm_back(ng, second_gain, norm2, scale2)
-    resid_grad = grad + back2
-    mg = resid_grad.astype(BF)
-    mix_bias_grad = jnp.sum(mg.astype(F32), axis=0)
-
-    mg_all = in_order(mg, swap(mg, 1))
+
     ag_b = dot(mg_all, wm_far, NT).astype(BF)
     dqkv_b, sums_b = attn_bwd(qkv_b, ag_b, segc, seg)
     qkv_grad_b = dot(rows1, dqkv_b, TN).astype(BF)
@@ -587,7 +690,7 @@
     dqkv_a, sums_a = attn_bwd(qkv_a, ag_a, segc, seg)
     qkv_back, mix_back, dqkv_a, br_got = lax.optimization_barrier((qkv_back, mix_back, dqkv_a, br_got))
 
-    branch = near_sum(br0) + br_got.astype(F32)
+    branch = br_near.astype(F32) + br_got.astype(F32)
     block_out = (resid + branch + reduce_bias).astype(BF)
 
     n1g_other = dot(other_rows(dqkv_b), wq_far, NT) + dot(other_rows(dqkv_a), wq, NT)
@@ -596,13 +699,12 @@
     back1, first_gain_grad, first_shift_grad = norm_back(n1g, first_gain, norm1, scale1)
     in_grad = resid_grad + back1
 
-    def over_tensor(parts):
-        a = jnp.stack(parts)
+    def over_tensor(a):
         a = a + swap(a, 1)
         return a + swap(a, 2)
 
-    early = over_tensor([mix_bias_grad, second_gain_grad, second_shift_grad, reduce_bias_grad])
-    late = over_tensor([first_gain_grad, first_shift_grad])
+    early = over_tensor(sums2)
+    late = over_tensor(jnp.stack([first_gain_grad, first_shift_grad]))
 
     mix_grad = (dot(att_a, mg_all, TN) + mix_back.astype(F32)).astype(BF)
     qkv_grad = (dot(rows1, dqkv_a, TN) + qkv_back.astype(F32)).astype(BF)
@@ -612,7 +714,7 @@
         [
             late,
             early,
-            expand_bias_grad.reshape(1, units),
+            unit_sums,
             jnp.pad(qv_bias_grad, ((0, 0), (0, width - 2 * cols))),
         ],
         axis=0,

time: 420 us -> 422 us (level)
  Pallas kernels: 159 us -> 189 us
  other arithmetic: 34.7 us -> 16.6 us
  matrix products: 52.4 us -> 40.4 us
  waiting for transfers between devices: 94.1 us -> 103 us
    pallas_call x2 -> x1, Pallas kernels: 30 us -> 59.7 us  [ff(): pl.pallas_call(ff_kernel, in_specs=[vmem] * 7, out_specs=[vmem] * 8, out_...]
    reduce_scatter x1, waiting for transfers between devices: 0.02 us -> 19.2 us  [body(): lax.psum_scatter(expand_grad, 'dp', scatter_dimension=0, tiled=True)]
    ppermute x26 -> x17, waiting for transfers between devices: 83.5 us -> 65.1 us  [swap(): return lax.ppermute(a, 'tensor', [(i, i ^ bit) for i in range(4)])]
    dot_general x18 -> x16, matrix products: 52.4 us -> 40.4 us  [dot(): return lax.dot_general(a, b, dims, preferred_element_type=F32)]
    all_gather x1, waiting for transfers between devices: 10.4 us -> 19.1 us  [body(): low = lax.all_gather(piece, 'dp', axis=0, tiled=True)]
    convert_element_type x3 -> x0, other arithmetic: 8.32 us -> none  [the longest x2 5.71 us: across(): return (far[:rows].astype(F32) + swap(far[rows:], 1).astype(F32)).astype(BF)]
    reduce_sum x2 -> x0, other arithmetic: 7.92 us -> none  [the longest x1 4.27 us: body(): mix_bias_grad = jnp.sum(mg.astype(F32), axis=0)]
    unnamed x135 -> x112, local copies, waits for them, and re-layouts: 16.3 us -> 23.4 us
  transfers between devices with their start and end apart: 29 -> 20, of which waited for: 11 -> 7; matrix products, arithmetic and copies ran while one was open for 20% -> 17% of each run, Pallas kernels for 12% -> 11%
where the time goes in v2:
time: 422 us; the launch traced here: 418 us
  Pallas kernels  189 us (45%)
  waiting for transfers between devices  103 us (24%)
  matrix products  40.4 us (10%)
  local copies, waits for them, and re-layouts  38.3 us (9%)
  other arithmetic  16.6 us (4%)
  starting transfers between devices  15.7 us (4%)
  between operations  14.9 us (4%)
    pallas_call x1, Pallas kernels, ring_sum(): pl.pallas_call(functools.partial(ring_kernel, n), in_specs=[vmem, vmem, a...  84.4 us
    ppermute x17, waiting for transfers between devices, swap(): return lax.ppermute(a, 'tensor', [(i, i ^ bit) for i in range(4)])  65.1 us
    pallas_call x1, Pallas kernels, ff(): pl.pallas_call(ff_kernel, in_specs=[vmem] * 7, out_specs=[vmem] * 8, out_...  59.7 us
    dot_general x16, matrix products, dot(): return lax.dot_general(a, b, dims, preferred_element_type=F32)  40.4 us
    pallas_call x2, Pallas kernels, attn_bwd(): pl.pallas_call(functools.partial(attn_bwd_kernel, blocks, pairs), grid=(p...  26.9 us
    unnamed x112, local copies, waits for them, and re-layouts  23.4 us
    reduce_scatter x1, waiting for transfers between devices, body(): lax.psum_scatter(expand_grad, 'dp', scatter_dimension=0, tiled=True)  19.2 us
    all_gather x1, waiting for transfers between devices, body(): low = lax.all_gather(piece, 'dp', axis=0, tiled=True)  19.1 us
  transfers between devices with their start and end apart: 20, of which 7 were waited for; matrix products, arithmetic and copies ran while one was open for 17% of the time, Pallas kernels for 11%

profile of v2, /device:TPU:0, one launch (start us, length us, event | category | flops | bytes accessed | tf_op | source)
XLA Modules:
  0.0 418.3 jit_solution(9700784747732441425)
XLA Ops:
  7.2 3.0 collective-permute-start
  10.4 1.1 fusion.38
  11.8 1.8 copy.49
  13.8 1.9 collective-permute-start.2
  16.5 1.4 fusion.7
  18.3 21.0 %collective-permute-done.2 = bf16[64,1024]{0,1:T(8,128)(2,1)S(1)} collective-permute-done((bf16[64,1024]{0,1:T(8,128)(2,1)S(1)}, bf16[64,1024]{0,1:T(8,128)(2,1)S(1)}, u32[]{:S(2)}, u32[]{:S(2)}) %collective-permute-start.2) | collective-permute-done | bytes 131104 | tf_op jit(solution)/shard_map/ppermute | solution.py:31
  39.3 0.8 copy.53
  40.7 2.3 constant_dynamic-update-slice_fusion.1
  42.9 1.0 pad_maximum_fusion.2
  44.3 1.8 collective-permute-start.1
  46.2 4.5 %add_convert_fusion.2.q_ref.k_ref.v_ref = bf16[1024,768]{1,0:T(8,128)(2,1)S(1)} fusion(bf16[1024,768]{0,1:T(8,128)(2,1)} %bitcast.64, f32[768]{0:T(1024)S(1)} %get-tuple-element.124, bf16[512,1024]{1,0:T(8,128)(2,1)} %collective-permute-done.3, bf16[512,1024]{1,0:T(8,128)(2,1)} %fusion.7, pred[]{:T(512)S(6)} %eq.5), kind=kOutput, calls=%fused_computation.2 | convolution fusion | flops 1621622784 | bytes 5245953 | tf_op jit(solution)/shard_map/dot_general | solution.py:23
  50.8 8.9 %attn_fwd.2 = bf16[1024,256]{1,0:T(8,128)(2,1)S(1)} custom-call(s32[1024,1]{1,0:T(8,128)S(1)} %copy.55.segc_ref, s32[1,1024]{1,0:T(1,128)S(1)} %constant_dynamic-slice_fusion.segr_ref, bf16[1024,768]{1,0:T(8,128)(2,1)S(1)} %add_convert_fusion.2.q_ref.k_ref.v_ref, bf16[1024,768]{1,0:T(8,128)(2,1)S(1)} %add_convert_fusion.2.q_ref.k_ref.v_ref, ...), custom_call_target="tpu_custom_call" | custom-call | flops 1073741824 | bytes 3145728 | tf_op jit(solution)/shard_map/attn_fwd/pallas_call | solution.py:82
  59.7 0.8 copy-done.2
  60.5 2.3 constant_dynamic-update-slice_fusion
  62.7 19.1 %all-gather.2.cloned.1.call-done = bf16[512,1024]{1,0:T(8,128)(2,1)} async-done(((bf16[64,1024]{1,0:T(8,128)(2,1)}), bf16[512,1024]{1,0:T(8,128)(2,1)}) %all-gather.2.cloned.1.call-update) | async-done | bytes 1048592 | tf_op jit(solution)/shard_map/all_gather | solution.py:643
  81.8 1.1 slice-done
  83.3 0.9 reshape.151
  84.1 1.0 slice.114
  85.2 0.9 reshape.150
  86.1 1.2 slice.112
  87.6 4.7 %add_convert_fusion.1.q_ref.k_ref.v_ref = bf16[1024,768]{1,0:T(8,128)(2,1)S(1)} fusion(bf16[1024,768]{0,1:T(8,128)(2,1)S(1)} %pad_maximum_fusion.1, f32[768]{0:T(1024)S(1)} %get-tuple-element.123, bf16[512,1024]{1,0:T(8,128)(2,1)} %collective-permute-done.3, bf16[512,1024]{1,0:T(8,128)(2,1)} %fusion.7, pred[]{:T(512)S(6)} %eq.5), kind=kOutput, calls=%fused_computation.1 | convolution fusion | flops 1621622784 | bytes 5245953 | tf_op jit(solution)/shard_map/dot_general | solution.py:23
  92.4 9.1 %attn_fwd.3 = bf16[1024,256]{1,0:T(8,128)(2,1)S(1)} custom-call(s32[1024,1]{1,0:T(8,128)S(1)} %copy-done.6, s32[1,1024]{1,0:T(1,128)S(1)} %constant_dynamic-slice_fusion.segr_ref, bf16[1024,768]{1,0:T(8,128)(2,1)S(1)} %add_convert_fusion.1.q_ref.k_ref.v_ref, bf16[1024,768]{1,0:T(8,128)(2,1)S(1)} %add_convert_fusion.1.q_ref.k_ref.v_ref, ...), custom_call_target="tpu_custom_call" | custom-call | flops 1073741824 | bytes 3145728 | tf_op jit(solution)/shard_map/attn_fwd/pallas_call | solution.py:82
  102.5 1.9 slice_dynamic-update-slice_fusion.3
  104.4 1.9 slice_dynamic-update-slice_fusion.2
  106.3 1.9 slice_dynamic-update-slice_fusion.1
  108.1 2.0 slice_dynamic-update-slice_fusion.og_ref
  110.6 0.8 fusion.42
  112.1 1.4 add_convert_fusion.5.n2_ref
  113.5 59.7 %ff.1 = (f32[512,1024]{1,0:T(8,128)}, bf16[1024,1024]{1,0:T(8,128)(2,1)}, bf16[1024,1024]{1,0:T(8,128)(2,1)}, bf16[1024,1024]{1,0:T(8,128)(2,1)}, bf16[512,1024]...) custom-call(bf16[512,1024]{1,0:T(8,128)(2,1)} %add_convert_fusion.5.n2_ref, ...), custom_call_target="tpu_custom_call" | custom-call | tf_op jit(solution)/shard_map/ff/pallas_call | solution.py:371
  173.7 2.5 convolution_convert_fusion.3.g_ref
  176.2 13.4 %attn_bwd.2 = (bf16[1024,768]{1,0:T(8,128)(2,1)S(1)}, f32[2,256]{1,0:T(2,128)S(1)}) custom-call(s32[1024,1]{1,0:T(8,128)S(1)} %copy-done.7, s32[1,1024]{1,0:T(1,128)S(1)} %constant_dynamic-slice_fusion.segr_ref, bf16[1024,768]{1,0:T(8,128)(2,1)S(1)} %add_convert_fusion.1.q_ref.k_ref.v_ref, bf16[1024,768]{1,0:T(8,128)(2,1)S(1)} %add_convert_fusion.1.q_ref.k_ref.v_ref, ...), custom_call_target="tpu_custom_call" | custom-call | flops 3221225472 | bytes 4718592 | tf_op jit(solution)/shard_map/attn_bwd/pallas_call | solution.py:160
  189.6 6.1 %convolution_convert_fusion = bf16[1024,768]{1,0:T(8,128)(2,1)} fusion(bf16[1024,768]{1,0:T(8,128)(2,1)S(1)} %get-tuple-element.45, bf16[512,1024]{1,0:T(8,128)(2,1)} %collective-permute-done.3, bf16[512,1024]{1,0:T(8,128)(2,1)} %fusion.7, pred[]{:T(512)S(6)} %eq.5), kind=kOutput, calls=%fused_computation.31 | convolution fusion | flops 1620836352 | bytes 5242881 | tf_op jit(solution)/shard_map/dot_general | solution.py:23
  195.7 1.5 collective-permute-start.8
  197.2 1.5 convolution_convert_fusion.2
  199.3 1.5 collective-permute-start.9
  200.8 0.5 collective-permute-start.10
  201.4 3.9 fusion.16
  205.2 2.3 fusion.19
  207.5 0.7 convolution_convert_fusion.1.g_ref
  208.6 13.5 %attn_bwd.3 = (bf16[1024,768]{1,0:T(8,128)(2,1)S(1)}, f32[2,256]{1,0:T(2,128)S(1)}) custom-call(s32[1024,1]{1,0:T(8,128)S(1)} %copy-done.8, s32[1,1024]{1,0:T(1,128)S(1)} %constant_dynamic-slice_fusion.segr_ref, bf16[1024,768]{1,0:T(8,128)(2,1)S(1)} %add_convert_fusion.2.q_ref.k_ref.v_ref, bf16[1024,768]{1,0:T(8,128)(2,1)S(1)} %add_convert_fusion.2.q_ref.k_ref.v_ref, ...), custom_call_target="tpu_custom_call" | custom-call | flops 3221225472 | bytes 4718592 | tf_op jit(solution)/shard_map/attn_bwd/pallas_call | solution.py:160
  222.1 1.5 collective-permute-start.15
  223.7 9.6 %collective-permute-done.16 = f32[2,256]{1,0:T(2,128)S(1)} collective-permute-done((f32[2,256]{1,0:T(2,128)S(1)}, f32[2,256]{1,0:T(2,128)S(1)}, u32[]{:S(2)}, u32[]{:S(2)}) %collective-permute-start.16) | collective-permute-done | bytes 2080 | tf_op jit(solution)/shard_map/ppermute | solution.py:31
  233.2 33.5 %collective-permute-done.15 = f32[4,1024]{1,0:T(4,128)S(1)} collective-permute-done((f32[4,1024]{1,0:T(4,128)S(1)}, f32[4,1024]{1,0:T(4,128)S(1)}, u32[]{:S(2)}, u32[]{:S(2)}) %collective-permute-start.15) | collective-permute-done | bytes 16416 | tf_op jit(solution)/shard_map/ppermute | solution.py:31
  266.8 2.7 fusion.14
  269.5 2.2 concatenate.48
  271.7 2.6 add_convert_fusion.3
  274.4 4.9 %add_convert_fusion = bf16[1024,768]{1,0:T(8,128)(2,1)S(1)} fusion(bf16[1024,768]{1,0:T(8,128)(2,1)} %collective-permute-done.8, bf16[1024,768]{1,0:T(8,128)(2,1)S(1)} %get-tuple-element.51, bf16[512,1024]{1,0:T(8,128)(2,1)} %collective-permute-done.3, bf16[512,1024]{1,0:T(8,128)(2,1)} %fusion.7, pred[]{:T(512)S(6)} %eq.5), kind=kOutput, calls=%fused_computation | convolution fusion | flops 1622409216 | bytes 6815745 | tf_op jit(solution)/shard_map/dot_general | solution.py:23
  279.6 1.3 copy-done.21
  281.2 2.9 add_convert_fusion.4
  284.1 1.8 fusion.12
  286.4 0.8 collective-permute-done.12
  287.2 1.5 collective-permute-start.13
  288.8 2.0 fusion.11
  291.1 19.2 %reduce-scatter.5.cloned.1.call-done = bf16[128,1024]{1,0:T(8,128)(2,1)} async-done(((bf16[1024,1024]{1,0:T(8,128)(2,1)}), bf16[128,1024]{1,0:T(8,128)(2,1)}) %reduce-scatter.5.cloned.1.call-update) | async-done | bytes 262160 | tf_op jit(solution)/shard_map/reduce_scatter | solution.py:680
  310.3 0.9 copy-done.14
  311.2 0.9 copy-done.15
  312.2 84.4 %ring_sum.1 = (bf16[8,2,64,1024]{3,2,1,0:T(8,128)(2,1)S(1)}, f32[8,1,1024]{2,1,0:T(1,128)S(1)}, bf16[8,2,64,1024]{3,2,1,0:T(8,128)(2,1)S(1)}, bf16[8,2,64,1024]{3,2,1,0:T(8,128)(2,1)S(1)}) custom-call(bf16[8,2,64,1024]{3,2,1,0:T(8,128)(2,1)S(1)} %pad_maximum_fusion.x_ref, f32[8,1,1024]{2,1,0:T(1,128)S(1)} %reshape.154.small_ref, ...), custom_call_target="tpu_custom_call" | custom-call | tf_op jit(solution)/shard_map/ring_sum/pallas_call | solution.py:538
  396.6 0.7 fusion.39
  398.0 0.7 copy-done.13
  398.7 0.6 reshape_squeeze.3
  399.3 1.6 copy.65
  400.9 1.3 reshape.166
  402.2 3.2 copy.61
  405.4 6.2 %bitcast_convert_fusion = (f32[1024,1024]{1,0:T(8,128)}, f32[1024,1024]{1,0:T(8,128)}) fusion(bf16[8,2,64,1024]{3,2,1,0:T(8,128)(2,1)S(1)} %copy-done.12, bf16[8,2,64,1024]{3,2,1,0:T(8,128)(2,1)} %copy-done.13), kind=kLoop, calls=%fused_computation.22 | loop fusion | flops 2097152 | bytes 12582912 | tf_op jit(solution)/shard_map/convert_element_type | solution.py:736
  (171 shorter events, 8.9 us)
Async XLA Ops:
  7.2 33.5 %copy-start = (s32[2,1024]{1,0:T(2,128)S(1)}, s32[2,1024]{1,0:T(2,128)}, u32[]{:S(2)}) copy-start(s32[2,1024]{1,0:T(2,128)} %param.16) | copy-start | bytes 24580
  7.2 74.6 %all-gather.2.cloned.1.call-start = ((), (), s32[]{:S(2)}) async-start(), calls=%async_computation.2 | async-start | bytes 1179648 | tf_op jit(solution)/shard_map/all_gather | solution.py:643
  7.2 37.0 %collective-permute-start = (bf16[512,1024]{1,0:T(8,128)(2,1)}, bf16[512,1024]{1,0:T(8,128)(2,1)}, u32[]{:S(2)}, u32[]{:S(2)}) collective-permute-start(bf16[512,1024]{1,0:T(8,128)(2,1)} %param.29), channel_id=1, source_target_pairs={{0,2},{1,3},{2,0},{3,1},{4,6},{5,7},{6,4},{7,5},{8,10},{9,11},{10,... | collective-permute-start | bytes 3145736 | tf_op jit(solution)/shard_map/ppermute | solution.py:31
  10.3 50.2 %collective-permute-start.6 = (bf16[512,1024]{1,0:T(8,128)(2,1)}, bf16[512,1024]{1,0:T(8,128)(2,1)}, u32[]{:S(2)}, u32[]{:S(2)}) collective-permute-start(bf16[512,1024]{1,0:T(8,128)(2,1)} %param.29), channel_id=1, source_target_pairs={{0,1},{1,0},{2,3},{3,2},{4,5},{5,4},{6,7},{7,6},{8,9},{9,8},{10,11... | collective-permute-start | bytes 3145736 | tf_op jit(solution)/shard_map/ppermute | solution.py:31
  10.3 35.8 %collective-permute-start.4 = (f32[2,256]{1,0:T(2,128)}, f32[2,256]{1,0:T(2,128)S(1)}, u32[]{:S(2)}, u32[]{:S(2)}) collective-permute-start(f32[2,256]{1,0:T(2,128)} %param.20), channel_id=1, source_target_pairs={{0,2},{1,3},{2,0},{3,1},{4,6},{5,7},{6,4},{7,5},{8,10},{9,11},{10,... | collective-permute-start | bytes 6152 | tf_op jit(solution)/shard_map/ppermute | solution.py:31
  11.7 4.1 copy-start.22
  13.6 4.3 %copy-start.30 = (bf16[1024,3,256]{0,2,1:T(8,128)(2,1)}, bf16[1024,3,256]{0,2,1:T(8,128)(2,1)S(1)}, u32[]{:S(2)}) copy-start(bf16[1024,3,256]{0,2,1:T(8,128)(2,1)S(1)} %copy.49) | copy-start | bytes 4718596
  13.6 2.8 copy-start.41
  13.6 2.8 copy-start.43
  13.8 25.5 %collective-permute-start.2 = (bf16[64,1024]{0,1:T(8,128)(2,1)S(1)}, bf16[64,1024]{0,1:T(8,128)(2,1)S(1)}, u32[]{:S(2)}, u32[]{:S(2)}) collective-permute-start(bf16[64,1024]{0,1:T(8,128)(2,1)S(1)} %pad_maximum_fusion.4), channel_id=1, source_target_pairs={{0,2},{1,3},{2,0},{3,1},{4,6},{5,7},{6,4},{7,5},{8,10},{9,11},{10,... | collective-permute-start | bytes 393224 | tf_op jit(solution)/shard_map/ppermute | solution.py:31
  17.9 28.3 %collective-permute-start.3 = (bf16[512,1024]{1,0:T(8,128)(2,1)}, bf16[512,1024]{1,0:T(8,128)(2,1)}, u32[]{:S(2)}, u32[]{:S(2)}) collective-permute-start(bf16[512,1024]{1,0:T(8,128)(2,1)} %fusion.7), channel_id=1, source_target_pairs={{0,1},{1,0},{2,3},{3,2},{4,5},{5,4},{6,7},{7,6},{8,9},{9,8},{10,11... | collective-permute-start | bytes 3145736 | tf_op jit(solution)/shard_map/ppermute | solution.py:31
  40.1 251.0 %reduce-scatter.3.cloned.1.call-start = ((), (), s32[]{:S(2)}) async-start(), calls=%async_computation.3 | async-start | bytes 2359296 | tf_op jit(solution)/shard_map/reduce_scatter | solution.py:679
  40.7 3.3 copy-start.48
  44.3 6.5 %copy-start.5 = (s32[1024,1]{1,0:T(8,128)}, s32[1024,1]{1,0:T(8,128)S(1)}, u32[]{:S(2)}) copy-start(s32[1024,1]{1,0:T(8,128)S(1)} %copy.55.segc_ref) | copy-start | bytes 12292
  44.3 39.8 %collective-permute-start.1 = (bf16[512,1024]{0,1:T(8,128)(2,1)}, bf16[512,1024]{0,1:T(8,128)(2,1)}, u32[]{:S(2)}, u32[]{:S(2)}) collective-permute-start(bf16[512,1024]{0,1:T(8,128)(2,1)} %pad_maximum_fusion.2), channel_id=1, source_target_pairs={{0,2},{1,3},{2,0},{3,1},{4,6},{5,7},{6,4},{7,5},{8,10},{9,11},{10,... | collective-permute-start | bytes 3145736 | tf_op jit(solution)/shard_map/ppermute | solution.py:31
  46.1 58.3 %collective-permute-start.7 = (bf16[512,1024]{1,0:T(8,128)(2,1)}, bf16[512,1024]{1,0:T(8,128)(2,1)}, u32[]{:S(2)}, u32[]{:S(2)}) collective-permute-start(bf16[512,1024]{1,0:T(8,128)(2,1)} %collective-permute-done), channel_id=1, source_target_pairs={{0,1},{1,0},{2,3},{3,2},{4,5},{5,4},{6,7},{7,6},{8,9},{9,8},{10,11... | collective-permute-start | bytes 3145736 | tf_op jit(solution)/shard_map/ppermute | solution.py:31
  81.8 1.4 slice-start.1
  86.1 1.4 copy-start.37
  86.1 1.5 copy-start.38
  87.6 4.8 %copy-start.35 = (bf16[1024,768]{0,1:T(8,128)(2,1)}, bf16[1024,768]{0,1:T(8,128)(2,1)S(1)}, u32[]{:S(2)}) copy-start(bf16[1024,768]{0,1:T(8,128)(2,1)S(1)} %pad_maximum_fusion.1) | copy-start | bytes 4718596
  87.6 22.9 %copy-start.29 = (bf16[256,1024]{1,0:T(8,128)(2,1)}, bf16[256,1024]{1,0:T(8,128)(2,1)S(1)}, u32[]{:S(2)}) copy-start(bf16[256,1024]{1,0:T(8,128)(2,1)S(1)} %pad_maximum_fusion.3) | copy-start | bytes 1572868
  87.6 4.8 %copy-start.6 = (s32[1024,1]{1,0:T(8,128)S(1)}, s32[1024,1]{1,0:T(8,128)}, u32[]{:S(2)}) copy-start(s32[1024,1]{1,0:T(8,128)} %copy-done.5) | copy-start | bytes 12292
  92.4 9.1 %copy-start.3 = (bf16[1024,256]{1,0:T(8,128)(2,1)S(1)}, bf16[1024,256]{1,0:T(8,128)(2,1)}, u32[]{:S(2)}) copy-start(bf16[1024,256]{1,0:T(8,128)(2,1)} %copy-done.2) | copy-start | bytes 1572868
  92.4 9.1 %copy-start.27 = (bf16[256,1024]{1,0:T(8,128)(2,1)S(1)}, bf16[256,1024]{1,0:T(8,128)(2,1)}, u32[]{:S(2)}) copy-start(bf16[256,1024]{1,0:T(8,128)(2,1)} %param.21) | copy-start | bytes 1572868
  101.5 9.0 %copy-start.9 = (bf16[1024,256]{1,0:T(8,128)(2,1)}, bf16[1024,256]{1,0:T(8,128)(2,1)S(1)}, u32[]{:S(2)}) copy-start(bf16[1024,256]{1,0:T(8,128)(2,1)S(1)} %attn_fwd.3) | copy-start | bytes 1572868
  102.4 8.1 %collective-permute-start.5 = (bf16[512,1024]{1,0:T(8,128)(2,1)S(1)}, bf16[512,1024]{1,0:T(8,128)(2,1)S(1)}, u32[]{:S(2)}, u32[]{:S(2)}) collective-permute-start(bf16[512,1024]{1,0:T(8,128)(2,1)S(1)} %add_convert_fusion.6), channel_id=1, source_target_pairs={{0,1},{1,0},{2,3},{3,2},{4,5},{5,4},{6,7},{7,6},{8,9},{9,8},{10,11... | collective-permute-start | bytes 3145736 | tf_op jit(solution)/shard_map/ppermute | solution.py:31
  108.1 2.4 copy-start.23
  108.1 2.4 copy-start.44
  111.4 2.1 copy-start.20
  173.2 137.1 %reduce-scatter.5.cloned.1.call-start = ((), (), s32[]{:S(2)}) async-start(), calls=%async_computation.4 | async-start | bytes 2359296 | tf_op jit(solution)/shard_map/reduce_scatter | solution.py:680
  173.7 2.5 copy-start.7
  189.5 6.2 %copy-start.18 = (bf16[1024,768]{1,0:T(8,128)(2,1)}, bf16[1024,768]{1,0:T(8,128)(2,1)S(1)}, u32[]{:S(2)}) copy-start(bf16[1024,768]{1,0:T(8,128)(2,1)S(1)} %get-tuple-element.45) | copy-start | bytes 4718596
  189.6 7.6 %copy-start.10 = (bf16[1024,256]{1,0:T(8,128)(2,1)S(1)}, bf16[1024,256]{1,0:T(8,128)(2,1)}, u32[]{:S(2)}) copy-start(bf16[1024,256]{1,0:T(8,128)(2,1)} %copy-done.9) | copy-start | bytes 1572868
  189.6 7.6 %copy-start.25 = (bf16[1024,1024]{1,0:T(8,128)(2,1)S(1)}, bf16[1024,1024]{1,0:T(8,128)(2,1)}, u32[]{:S(2)}) copy-start(bf16[1024,1024]{1,0:T(8,128)(2,1)} %get-tuple-element.46) | copy-start | bytes 6291460
  195.7 3.6 copy-start.42
  195.7 71.1 %collective-permute-start.8 = (bf16[1024,768]{1,0:T(8,128)(2,1)}, bf16[1024,768]{1,0:T(8,128)(2,1)}, u32[]{:S(2)}, u32[]{:S(2)}) collective-permute-start(bf16[1024,768]{1,0:T(8,128)(2,1)} %convolution_convert_fusion), channel_id=1, source_target_pairs={{0,2},{1,3},{2,0},{3,1},{4,6},{5,7},{6,4},{7,5},{8,10},{9,11},{10,... | collective-permute-start | bytes 4718600 | tf_op jit(solution)/shard_map/ppermute | solution.py:31
  197.2 4.1 copy-start.19
  198.7 34.5 %collective-permute-start.16 = (f32[2,256]{1,0:T(2,128)S(1)}, f32[2,256]{1,0:T(2,128)S(1)}, u32[]{:S(2)}, u32[]{:S(2)}) collective-permute-start(f32[2,256]{1,0:T(2,128)S(1)} %get-tuple-element.57), channel_id=1, source_target_pairs={{0,2},{1,3},{2,0},{3,1},{4,6},{5,7},{6,4},{7,5},{8,10},{9,11},{10,... | collective-permute-start | bytes 6152 | tf_op jit(solution)/shard_map/ppermute | solution.py:31
  199.3 22.8 %collective-permute-start.14 = (f32[4,1024]{1,0:T(4,128)S(1)}, f32[4,1024]{1,0:T(4,128)S(1)}, u32[]{:S(2)}, u32[]{:S(2)}) collective-permute-start(f32[4,1024]{1,0:T(4,128)S(1)} %copy-done.42), channel_id=1, source_target_pairs={{0,1},{1,0},{2,3},{3,2},{4,5},{5,4},{6,7},{7,6},{8,9},{9,8},{10,11... | collective-permute-start | bytes 49160 | tf_op jit(solution)/shard_map/ppermute | solution.py:31
  199.3 67.5 %collective-permute-start.9 = (bf16[256,1024]{1,0:T(8,128)(2,1)}, bf16[256,1024]{1,0:T(8,128)(2,1)}, u32[]{:S(2)}, u32[]{:S(2)}) collective-permute-start(bf16[256,1024]{1,0:T(8,128)(2,1)} %convolution_convert_fusion.2), channel_id=1, source_target_pairs={{0,2},{1,3},{2,0},{3,1},{4,6},{5,7},{6,4},{7,5},{8,10},{9,11},{10,... | collective-permute-start | bytes 1572872 | tf_op jit(solution)/shard_map/ppermute | solution.py:31
  200.8 66.0 %collective-permute-start.10 = (bf16[512,1024]{1,0:T(8,128)(2,1)}, bf16[512,1024]{1,0:T(8,128)(2,1)}, u32[]{:S(2)}, u32[]{:S(2)}) collective-permute-start(bf16[512,1024]{1,0:T(8,128)(2,1)} %get-tuple-element.48), channel_id=1, source_target_pairs={{0,2},{1,3},{2,0},{3,1},{4,6},{5,7},{6,4},{7,5},{8,10},{9,11},{10,... | collective-permute-start | bytes 3145736 | tf_op jit(solution)/shard_map/ppermute | solution.py:31
  201.3 3.9 copy-start.36
  205.2 2.3 copy-start.26
  205.2 2.3 copy-start.28
  208.6 58.2 %copy-start.4 = (bf16[1024,256]{1,0:T(8,128)(2,1)S(1)}, bf16[1024,256]{1,0:T(8,128)(2,1)}, u32[]{:S(2)}) copy-start(bf16[1024,256]{1,0:T(8,128)(2,1)} %copy-done.2) | copy-start | bytes 1572868
  222.1 52.3 %copy-start.16 = (bf16[1024,768]{1,0:T(8,128)(2,1)}, bf16[1024,768]{1,0:T(8,128)(2,1)S(1)}, u32[]{:S(2)}) copy-start(bf16[1024,768]{1,0:T(8,128)(2,1)S(1)} %get-tuple-element.51) | copy-start | bytes 4718596
  222.1 44.6 %collective-permute-start.15 = (f32[4,1024]{1,0:T(4,128)S(1)}, f32[4,1024]{1,0:T(4,128)S(1)}, u32[]{:S(2)}, u32[]{:S(2)}) collective-permute-start(f32[4,1024]{1,0:T(4,128)S(1)} %add.184), channel_id=1, source_target_pairs={{0,2},{1,3},{2,0},{3,1},{4,6},{5,7},{6,4},{7,5},{8,10},{9,11},{10,... | collective-permute-start | bytes 49160 | tf_op jit(solution)/shard_map/ppermute | solution.py:31
  266.8 4.9 %copy-start.31 = (bf16[1024,3,256]{0,2,1:T(8,128)(2,1)S(1)}, bf16[1024,3,256]{0,2,1:T(8,128)(2,1)}, u32[]{:S(2)}) copy-start(bf16[1024,3,256]{0,2,1:T(8,128)(2,1)} %copy-done.30) | copy-start | bytes 4718596
  274.3 5.0 %copy-start.34 = (bf16[8,2,64,256]{3,2,1,0:T(8,128)(2,1)S(1)}, bf16[8,2,64,256]{3,2,1,0:T(8,128)(2,1)}, u32[]{:S(2)}) copy-start(bf16[8,2,64,256]{3,2,1,0:T(8,128)(2,1)} %concatenate.48) | copy-start | bytes 1572868
  274.3 9.7 %collective-permute-start.11 = (bf16[512,1024]{1,0:T(8,128)(2,1)S(1)}, bf16[512,1024]{1,0:T(8,128)(2,1)S(1)}, u32[]{:S(2)}, u32[]{:S(2)}) collective-permute-start(bf16[512,1024]{1,0:T(8,128)(2,1)S(1)} %add_convert_fusion.3), channel_id=1, source_target_pairs={{0,1},{1,0},{2,3},{3,2},{4,5},{5,4},{6,7},{7,6},{8,9},{9,8},{10,11... | collective-permute-start | bytes 3145736 | tf_op jit(solution)/shard_map/ppermute | solution.py:31
  279.3 1.6 copy-start.21
  279.3 1.9 copy-start.39
  279.3 1.9 copy-start.47
  279.3 4.7 %copy-start.49 = (f32[512,1024]{1,0:T(8,128)S(1)}, f32[512,1024]{1,0:T(8,128)}, u32[]{:S(2)}) copy-start(f32[512,1024]{1,0:T(8,128)} %fusion.19) | copy-start | bytes 6291460
  281.2 2.9 copy-start.17
  281.2 2.9 copy-start.24
  281.2 2.9 copy-start.32
  284.1 4.7 %copy-start.33 = (f32[512,1024]{1,0:T(8,128)S(1)}, f32[512,1024]{1,0:T(8,128)}, u32[]{:S(2)}) copy-start(f32[512,1024]{1,0:T(8,128)} %get-tuple-element.50) | copy-start | bytes 6291460
  285.9 1.3 collective-permute-start.12
  287.2 3.7 collective-permute-start.13
  288.8 2.2 copy-start.46
  396.6 2.1 copy-start.13
  402.2 3.2 copy-start.12
  405.4 6.2 %copy-start.1 = (s32[2,1024]{1,0:T(2,128)S(1)}, s32[2,1024]{1,0:T(2,128)}, u32[]{:S(2)}) copy-start(s32[2,1024]{1,0:T(2,128)} %param.16) | copy-start | bytes 24580
  (8 other events, 7.7 us)
Sparse Core Ops, SparseCore 0:
  40.2 41.5 all-gather.1
  173.3 66.6 reduce-scatter.2
  243.5 66.7 reduce-scatter.4
